TPU v7x, 32 devices: a whole 2x2x4 slice. The times are simulated.
32 devices in a mesh: dp: 8 (over z, y), frame: 4 (over x, core).
Axes of the slice: x: 2, y: 2, z: 4, core: 2. Of those that a mesh axis runs over, the one named last changes fastest.
Arguments:
- mel_frames: bfloat16 [16, 3008, 80], P('dp', 'frame'), may hold values from -6 to 6
- window_count: int32 [8], P('dp'), may hold values from 1 to 2, as said below
- stem_weight: bfloat16 [3, 80, 512], replicated, may hold values from -0.375 to 0.375
- stem_bias: float32 [512], replicated, may hold values from -1.5 to 1.5
- reduce_weight: bfloat16 [3, 512, 512], replicated, may hold values from -0.15625 to 0.15625
- reduce_bias: float32 [512], replicated, may hold values from -1.5 to 1.5
- first_gain: float32 [512], replicated, may hold values from 0.5 to 1.5
- first_shift: float32 [512], replicated, may hold values from -1.5 to 1.5
- query_weight: bfloat16 [512, 512], replicated, may hold values from -0.25 to 0.25
- query_bias: float32 [512], replicated, may hold values from -1.5 to 1.5
- key_weight: bfloat16 [512, 512], replicated, may hold values from -0.25 to 0.25
- value_weight: bfloat16 [512, 512], replicated, may hold values from -0.25 to 0.25
- value_bias: float32 [512], replicated, may hold values from -1.5 to 1.5
- output_weight: bfloat16 [512, 512], replicated, may hold values from -4 to 4
- output_bias: float32 [512], replicated, may hold values from -1.5 to 1.5
- second_gain: float32 [512], replicated, may hold values from 0.5 to 1.5
- second_shift: float32 [512], replicated, may hold values from -1.5 to 1.5
- hidden_weight: bfloat16 [512, 2048], replicated, may hold values from -0.25 to 0.25
- hidden_bias: float32 [2048], replicated, may hold values from -1.5 to 1.5
- return_weight: bfloat16 [2048, 512], replicated, may hold values from -0.125 to 0.125
- return_bias: float32 [512], replicated, may hold values from -1.5 to 1.5
- cotangent: bfloat16 [16, 1504, 512], P('dp', 'frame'), may hold values from -6 to 6
Outputs:
- layer_output: bfloat16 [16, 1504, 512], P('dp', 'frame')
- mel_gradient: float32 [16, 3008, 80], P('dp', 'frame')
- stem_weight_gradient: float32 [3, 80, 512], replicated
- stem_bias_gradient: float32 [512], replicated
- reduce_weight_gradient: float32 [3, 512, 512], replicated
- reduce_bias_gradient: float32 [512], replicated
- first_gain_gradient: float32 [512], replicated
- first_shift_gradient: float32 [512], replicated
- query_weight_gradient: float32 [512, 512], replicated
- query_bias_gradient: float32 [512], replicated
- key_weight_gradient: float32 [512, 512], replicated
- value_weight_gradient: float32 [512, 512], replicated
- value_bias_gradient: float32 [512], replicated
- output_weight_gradient: float32 [512, 512], replicated
- output_bias_gradient: float32 [512], replicated
- second_gain_gradient: float32 [512], replicated
- second_shift_gradient: float32 [512], replicated
- hidden_weight_gradient: float32 [512, 2048], replicated
- hidden_bias_gradient: float32 [2048], replicated
- return_weight_gradient: float32 [2048, 512], replicated
- return_bias_gradient: float32 [512], replicated
Inputs may be any that keep to these rules, and one draw needn't show every extreme that they name: `window_count`: slots of a data group at or beyond its count hold no window. Some group has exactly 2 windows and some group exactly 1.
All inputs are finite; a program needn't handle non-finite values.
Results may differ from a plain program's by a relative error of at most 0.013.
Values may be sent and summed in bfloat16 or wider, within the bound.
A program may use at most 192 MiB of HBM per device.

v0:
```python
import functools
import math

import jax
import jax.numpy as jnp
from jax import lax
from jax.experimental import pallas as pl
from jax.experimental.pallas import tpu as pltpu
from jax.sharding import PartitionSpec as P

HEADS = 8
EPS = 1e-05
F32 = jnp.float32
BF16 = jnp.bfloat16
PHI_SLOPE = 0.28
PHI_POLY = (
    0.1167294156016242,
    0.06622785593379492,
    0.27197610469464767,
    -0.24067367858721922,
    0.3920693507793772,
    -0.10632905941542621,
)


def phi_parts(v):
    size = jnp.abs(v)
    t = 1.0 / (1.0 + PHI_SLOPE * size)
    bell = jnp.exp(-0.5 * v * v)
    poly = PHI_POLY[5]
    for c in PHI_POLY[4::-1]:
        poly = poly * t + c
    tail = poly * t * bell
    cdf = jnp.where(v >= 0, 1.0 - tail, tail)
    return cdf, bell * (1.0 / math.sqrt(2.0 * math.pi))


def gelu(v):
    cdf, _ = phi_parts(v)
    return v * cdf


def gelu_slope(v):
    cdf, pdf = phi_parts(v)
    return cdf + v * pdf


def dot(left, right):
    return jnp.dot(left, right, preferred_element_type=F32)


def dot_t(left, right):
    return lax.dot_general(left, right, (((1,), (1,)), ((), ())), preferred_element_type=F32)


def outer(left, right):
    return lax.dot_general(left, right, (((0,), (0,)), ((), ())), preferred_element_type=F32)


def column_total(x):
    return jnp.sum(x.astype(F32), axis=0)


def norm_parts(x):
    centred = x - jnp.mean(x, axis=-1, keepdims=True)
    r = lax.rsqrt(jnp.mean(centred * centred, axis=-1, keepdims=True) + EPS)
    return centred * r, r


def norm_pull(xhat, r, gain, dy):
    dh = dy * gain
    inner = r * (
        dh
        - jnp.mean(dh, axis=-1, keepdims=True)
        - xhat * jnp.mean(dh * xhat, axis=-1, keepdims=True)
    )
    return inner, column_total(dy * xhat), column_total(dy)


def positions_of(first, count, width):
    half = width // 2
    step = math.log(10000.0) / (half - 1)
    rate = jnp.exp(-step * jnp.arange(half, dtype=F32))[None, :]
    fine = math.gcd(count, 16)
    coarse = count // fine
    a = (first + fine * jnp.arange(coarse, dtype=jnp.int32)).astype(F32)[:, None] * rate
    b = jnp.arange(fine, dtype=jnp.int32).astype(F32)[:, None] * rate
    sa, ca = jnp.sin(a)[:, None, :], jnp.cos(a)[:, None, :]
    sb, cb = jnp.sin(b)[None, :, :], jnp.cos(b)[None, :, :]
    both = jnp.concatenate([sa * cb + ca * sb, ca * cb - sa * sb], axis=2)
    return both.reshape(count, width)


def half_mask(shape, h, hd):
    lane = lax.broadcasted_iota(jnp.int32, shape, 1)
    return (lane >= h*hd) & (lane < (h+1)*hd)

MESH = pl.DeviceIdType.MESH


def group_peer(G, o):
    fr = lax.axis_index("frame")
    return (lax.axis_index("dp"), fr // G * G + lax.rem(lax.rem(fr, G) + o, G))


def greet(F):
    barrier = pltpu.get_barrier_semaphore()
    for o in range(1, F):
        pl.semaphore_signal(barrier, inc=1, device_id=group_peer(F, o), device_id_type=MESH)


def meet(F):
    greet(F)
    pl.semaphore_wait(pltpu.get_barrier_semaphore(), F - 1)


class Move:
    def __init__(self, gather, F, src, dst, sems):
        self.src, self.dst = src, dst
        self.send, self.recv, self.own = sems
        self.S = src.shape[0]
        S, G = self.S, F // src.shape[0]
        self.dp, self.fr = lax.axis_index("dp"), lax.axis_index("frame")
        over = [a * G + self.fr // S for a in range(S)]
        back = [lax.rem(self.fr, G) * S + a for a in range(S)]
        self.to, self.sender = (over, back) if gather else (back, over)
        self.place = lax.rem(self.fr, S) if gather else self.fr // G

    def far(self, a):
        return pltpu.make_async_remote_copy(
            src_ref=self.src.at[a],
            dst_ref=self.dst.at[self.place],
            send_sem=self.send.at[a],
            recv_sem=self.recv.at[self.place],
            device_id=(self.dp, self.to[a]),
            device_id_type=MESH,
        )

    def near(self, a):
        return pltpu.make_async_copy(self.src.at[a], self.dst.at[self.place], self.own.at[a])

    def start(self):
        for a in range(self.S):

            @pl.when(self.to[a] != self.fr)
            def _():
                self.far(a).start()

            @pl.when(self.to[a] == self.fr)
            def _():
                self.near(a).start()

    def wait(self):
        for a in range(self.S):

            @pl.when(self.to[a] != self.fr)
            def _():
                self.far(a).wait_send()

            @pl.when(self.to[a] == self.fr)
            def _():
                self.near(a).wait()

            @pl.when(self.sender[a] != self.fr)
            def _():
                landed = self.dst.at[a]
                pltpu.make_async_copy(landed, landed, self.recv.at[a]).wait()


def move_sems(S):
    return [pltpu.SemaphoreType.DMA((S,))] * 3


def lanes_of(pair):
    return pl.ds(pl.multiple_of(pair * 128, 128), 128)


def fwd_kernel(
    scale,
    hd,
    F,
    G,
    T,
    pairs,
    q_ref,
    k_own,
    v_own,
    c_ref,
    p_ref,
    o_ref,
    k_all,
    v_all,
    d_ref,
    s_ref,
    k_buf,
    v_buf,
    send_sem,
    recv_sem,
    own_sem,
    out_sem,
    *sems,
):
    per = 128 // hd
    pair, i = pl.program_id(0), pl.program_id(1)
    rows = k_own.shape[0]
    both = ((k_own, k_buf), (v_own, v_buf))
    kept = ((k_buf, k_all), (v_buf, v_all))

    def own_copy(n, p):
        src, dst = both[n]
        return pltpu.make_async_copy(
            src.at[:, lanes_of(p)], dst.at[pl.ds(0, rows), lanes_of(p)], own_sem.at[n, p]
        )

    def keep(n, p):
        src, dst = kept[n]
        return pltpu.make_async_copy(
            src.at[:, lanes_of(p)], dst.at[:, lanes_of(p)], out_sem.at[n, p]
        )

    def copy_to(n, p, o):
        src, dst = both[n]
        return pltpu.make_async_remote_copy(
            src_ref=src.at[:, lanes_of(p)],
            dst_ref=dst.at[pl.ds((G - o) * rows, rows), lanes_of(p)],
            send_sem=send_sem.at[n, p, o - 1],
            recv_sem=recv_sem.at[n, p, o - 1],
            device_id=group_peer(G, o),
            device_id_type=MESH,
        )

    @pl.when((pair == 0) & (i == 0))
    def _():
        for p in range(pairs):
            for n in range(2):
                own_copy(n, p).start()
        meet(F)
        for p in range(pairs):
            for n in range(2):
                for o in range(1, G):
                    copy_to(n, p, o).start()
        Move(True, F, c_ref, d_ref, sems).start()

    @pl.when(i == 0)
    def _():
        for n in range(2):
            own_copy(n, pair).wait()
            for o in range(1, G):
                copy_to(n, pair, o).wait_recv()
            keep(n, pair).start()

    k = k_buf[:, lanes_of(pair)]
    vt = v_buf[:, lanes_of(pair)].T
    outs = []
    for h in range(per):
        q = q_ref[...]
        q = jnp.where(half_mask(q.shape, h, hd), q, jnp.zeros_like(q))
        s_ref[h] = lax.dot_general(k, q, (((1,), (1,)), ((), ())), preferred_element_type=F32)
    for h in range(per):
        s = s_ref[h]
        if rows != T:
            at = lax.rem(lax.broadcasted_iota(jnp.int32, s.shape, 0), rows)
            s = jnp.where(at < T, s, -1e30)
        m = jnp.max(s, axis=0, keepdims=True)
        e = jnp.exp((s - m) * scale)
        l = jnp.sum(e, axis=0, keepdims=True)
        p = (e * (1.0 / l)).astype(BF16)
        p_ref[h] = p
        outs.append(jnp.dot(vt[h * hd : (h + 1) * hd], p, preferred_element_type=F32))
    o_ref[...] = jnp.concatenate(outs, axis=0).T

    @pl.when((pair == pairs - 1) & (i == pl.num_programs(1) - 1))
    def _():
        for p in range(pairs):
            for n in range(2):
                keep(n, p).wait()
                for o in range(1, G):
                    copy_to(n, p, o).wait_send()
        Move(True, F, c_ref, d_ref, sems).wait()


def attn_fwd(q, k, v, slots, scale, heads, QB, F, T):
    G = F // slots.shape[0]
    R, D = q.shape
    N = k.shape[0] * G
    hd = D // heads
    per = 128 // hd
    pairs = D // 128
    far = pl.BlockSpec(memory_space=pl.ANY)
    sems = pltpu.SemaphoreType.DMA((2, pairs, G - 1))
    return pl.pallas_call(
        functools.partial(fwd_kernel, scale, hd, F, G, T, pairs),
        grid=(pairs, R // QB),
        in_specs=[pl.BlockSpec((QB, 128), lambda p, i: (i, p)), far, far, far],
        out_specs=[
            pl.BlockSpec((per, N, QB), lambda p, i: (p, 0, i)),
            pl.BlockSpec((QB, 128), lambda p, i: (i, p)),
            far,
            far,
            far,
        ],
        out_shape=[
            jax.ShapeDtypeStruct((heads, N, R), BF16),
            jax.ShapeDtypeStruct((R, D), F32),
            jax.ShapeDtypeStruct((N, D), BF16),
            jax.ShapeDtypeStruct((N, D), BF16),
            jax.ShapeDtypeStruct(slots.shape, slots.dtype),
        ],
        scratch_shapes=[
            pltpu.VMEM((per, N, QB), F32),
            pltpu.VMEM((N, D), BF16),
            pltpu.VMEM((N, D), BF16),
            sems,
            sems,
            pltpu.SemaphoreType.DMA((2, pairs)),
            pltpu.SemaphoreType.DMA((2, pairs)),
        ]
        + move_sems(slots.shape[0]),
        compiler_params=pltpu.CompilerParams(
            collective_id=1, has_side_effects=True, vmem_limit_bytes=60 << 20
        ),
    )(q, k, v, slots)


def bwd_kernel(
    scale,
    hd,
    F,
    G,
    pairs,
    q_ref,
    do_ref,
    o_ref,
    k_ref,
    v_ref,
    p_ref,
    y_ref,
    dq_ref,
    dk_ref,
    dv_ref,
    z_ref,
    dp_ref,
    kt_ref,
    acc_ref,
    got_ref,
    send_sem,
    recv_sem,
    *sems,
):
    per = 128 // hd
    pair, i = pl.program_id(0), pl.program_id(1)
    slot = lax.rem(pair, 2)
    rows = dk_ref.shape[0]

    def copy_to(n, p, o):
        return pltpu.make_async_remote_copy(
            src_ref=acc_ref.at[lax.rem(p, 2), n, pl.ds(o * rows, rows)],
            dst_ref=got_ref.at[p, n, o - 1],
            send_sem=send_sem.at[n, p, o - 1],
            recv_sem=recv_sem.at[n, p, o - 1],
            device_id=group_peer(G, o),
            device_id_type=MESH,
        )

    every = [(n, o) for n in range(2) for o in range(1, G)]

    @pl.when((pair == 0) & (i == 0))
    def _():
        meet(F)
        Move(False, F, y_ref, z_ref, sems).start()

    @pl.when((pair >= 2) & (i == 0))
    def _():
        for n, o in every:
            copy_to(n, pair - 2, o).wait_send()

    @pl.when(i == 0)
    def _():
        kt_ref[...] = k_ref[...].T
        acc_ref[slot] = jnp.zeros(acc_ref.shape[1:], F32)

    do = do_ref[...]
    q = q_ref[...]
    v = v_ref[...]
    prod = (do.astype(F32) * o_ref[...]).T
    for h in range(per):
        doh = jnp.where(half_mask(do.shape, h, hd), do, jnp.zeros_like(do))
        dp_ref[h] = lax.dot_general(v, doh, (((1,), (1,)), ((), ())), preferred_element_type=F32)
    dqs = []
    for h in range(per):
        doh = jnp.where(half_mask(do.shape, h, hd), do, jnp.zeros_like(do))
        qh = jnp.where(half_mask(q.shape, h, hd), q, jnp.zeros_like(q))
        delta = jnp.sum(prod[h * hd : (h + 1) * hd], axis=0, keepdims=True)
        p = p_ref[h]
        ds = (p.astype(F32) * (dp_ref[h] - delta)).astype(BF16)
        acc_ref[slot, 1] += jnp.dot(p, doh, preferred_element_type=F32)
        acc_ref[slot, 0] += jnp.dot(ds, qh, preferred_element_type=F32)
        dqs.append(jnp.dot(kt_ref[h * hd : (h + 1) * hd], ds, preferred_element_type=F32))
    dq_ref[...] = (jnp.concatenate(dqs, axis=0) * scale).T.astype(BF16)

    def finish(p):
        for n, o in every:
            copy_to(n, p, o).wait_recv()
        for n, out, factor in ((0, dk_ref, scale), (1, dv_ref, 1.0)):
            total = acc_ref[lax.rem(p, 2), n, pl.ds(0, rows)]
            for o in range(1, G):
                total = total + got_ref[p, n, o - 1]
            out[:, lanes_of(p)] = (total * factor).astype(BF16)

    ends = i == pl.num_programs(1) - 1

    @pl.when(ends & (pair >= 1))
    def _():
        finish(pair - 1)

    @pl.when(ends)
    def _():
        for n, o in every:
            copy_to(n, pair, o).start()

    @pl.when(ends & (pair == pairs - 1))
    def _():
        finish(pair)
        for p in range(max(pairs - 2, 0), pairs):
            for n, o in every:
                copy_to(n, p, o).wait_send()
        Move(False, F, y_ref, z_ref, sems).wait()


def attn_bwd(q, do, o, k, v, p, pieces, scale, heads, QB, F):
    G = F // pieces.shape[0]
    far = pl.BlockSpec(memory_space=pl.ANY)
    R, D = q.shape
    N = k.shape[0]
    hd = D // heads
    per = 128 // hd
    pairs = D // 128
    row = pl.BlockSpec((QB, 128), lambda p, i: (i, p))
    key = pl.BlockSpec((N, 128), lambda p, i: (0, p))
    near = pl.BlockSpec(memory_space=pltpu.VMEM)
    sems = pltpu.SemaphoreType.DMA((2, pairs, G - 1))
    own = jax.ShapeDtypeStruct((N // G, D), BF16)
    return pl.pallas_call(
        functools.partial(bwd_kernel, scale, hd, F, G, pairs),
        grid=(pairs, R // QB),
        in_specs=[row, row, row, key, key, pl.BlockSpec((per, N, QB), lambda p, i: (p, 0, i)), far],
        out_specs=[row, near, near, far],
        out_shape=[
            jax.ShapeDtypeStruct((R, D), BF16),
            own,
            own,
            jax.ShapeDtypeStruct(pieces.shape, pieces.dtype),
        ],
        scratch_shapes=[
            pltpu.VMEM((per, N, QB), F32),
            pltpu.VMEM((128, N), BF16),
            pltpu.VMEM((2, 2, N, 128), F32),
            pltpu.VMEM((pairs, 2, G - 1, N // G, 128), F32),
            sems,
            sems,
        ]
        + move_sems(pieces.shape[0]),
        compiler_params=pltpu.CompilerParams(
            collective_id=2, has_side_effects=True, vmem_limit_bytes=60 << 20
        ),
    )(q, do, o, k, v, p, pieces)


TILE = 512
LAG = 3
AHEAD = 3


def pick(c, values):
    out = values[0]
    for n in range(1, len(values)):
        if values[n] != values[n - 1]:
            out = jnp.where(c >= n, values[n], out)
    return out


def sum_kernel(sizes, F, used, plan, *refs):
    places, left_at, right_at, lefts, rights, n_in, n_out = plan
    in_refs, short_ref, piece_ref = refs[: n_in - 2], refs[n_in - 2], refs[n_in - 1]
    g_refs, slot_ref = refs[n_in : n_in + n_out - 1], refs[n_in + n_out - 1]
    refs = refs[n_in + n_out :]
    l_ref, m_ref, t_ref, w_ref, s_ref, r0, r1, r2, r3 = refs[:9]
    send_sem, recv_sem, load_sem, out_sem, *sems = refs[9:]
    t_ref[...] = jnp.zeros_like(t_ref)
    recv = (r0, r1, r2, r3)
    chunks = len(places)
    T = l_ref.shape[1]
    Y = sizes[2]
    dp = lax.axis_index("dp")
    fr = lax.axis_index("frame")
    z = dp // Y
    y = lax.rem(dp, Y)
    x = fr // 2
    core = lax.rem(fr, 2)
    first = core == 0
    me = (core, jnp.where(first, x, y), jnp.where(first, y, x), z)

    loads = []
    for buf, sources, base in ((l_ref, lefts, 0), (m_ref, rights, len(lefts))):
        for n, (which, col) in enumerate(sources):
            src = in_refs[which].at[pl.ds(0, T), pl.ds(col, TILE)]
            loads.append(pltpu.make_async_copy(src, buf.at[n], load_sem.at[base + n]))
    loads.append(
        pltpu.make_async_copy(short_ref, w_ref.at[chunks - 1], load_sem.at[len(lefts) + len(rights)])
    )
    due = [0] * len(loads)
    for n in range(len(lefts)):
        due[n] = left_at.index(n)
    for n in range(len(rights)):
        due[len(lefts) + n] = right_at.index(n)
    due[-1] = chunks - 1
    for n in sorted(range(len(loads)), key=lambda n: (due[n], n)):
        loads[n].start()

    def device(kind, p):
        if kind == 0:
            return (dp, x * 2 + p)
        if kind == 3:
            return (p * Y + y, fr)
        along_x = first if kind == 1 else jnp.logical_not(first)
        return (z * Y + jnp.where(along_x, y, p), jnp.where(along_x, p, x) * 2 + core)

    def peer(k, o):
        return lax.rem(me[k] + o, sizes[k])

    pairs = [(k, o) for k in range(4) for o in range(1, sizes[k])]
    barrier = pltpu.get_barrier_semaphore()
    for k, o in pairs:
        pl.semaphore_signal(barrier, inc=1, device_id=device(k, peer(k, o)), device_id_type=MESH)
    greet(F)
    pl.semaphore_wait(barrier, len(pairs) + F - 1)
    move = Move(False, F, piece_ref, slot_ref, sems)
    move.start()

    cut = [TILE]
    for k in range(4):
        cut.append(cut[-1] // sizes[k])
    split = cut[4] % 16 == 0
    if not split:
        cut[4] = cut[3]

    def start_of(level):
        at = 0
        for k in range(level):
            if k < 3 or split:
                at = at + me[k] * cut[k + 1]
        return pl.multiple_of(at, 16) if level else 0

    def scatter_copy(c, k, o):
        p = peer(k, o)
        at = start_of(k)
        if k < 3 or split:
            at = pl.multiple_of(at + p * cut[k + 1], 16)
        return pltpu.make_async_remote_copy(
            src_ref=w_ref.at[c, pl.ds(at, cut[k + 1])],
            dst_ref=recv[k].at[c, o - 1],
            send_sem=send_sem.at[c, k, o - 1],
            recv_sem=recv_sem.at[c, k, o - 1],
            device_id=device(k, p),
            device_id_type=MESH,
        )

    def gather_copy(c, k, o):
        here = s_ref.at[c, pl.ds(start_of(k + 1), cut[k + 1])]
        return pltpu.make_async_remote_copy(
            src_ref=here,
            dst_ref=here,
            send_sem=send_sem.at[c, 4 + k, o - 1],
            recv_sem=recv_sem.at[c, 4 + k, o - 1],
            device_id=device(k, peer(k, o)),
            device_id_type=MESH,
        )

    def out_copy(c):
        which, row, col = places[c]
        dst = g_refs[which].at[pl.ds(row, TILE), pl.ds(col, TILE)]
        return pltpu.make_async_copy(s_ref.at[c], dst, out_sem.at[c])

    def add(c, k):
        at = start_of(k + 1)
        dst = w_ref if k < 3 else s_ref
        step = math.gcd(cut[k + 1], 64)

        def body(i, _):
            r = pl.multiple_of(at + i * step, 16)
            total = w_ref[c, pl.ds(r, step)].astype(F32)
            for o in range(1, sizes[k]):
                total = total + recv[k][
                    c, o - 1, pl.ds(pl.multiple_of(i * step, 16), step)
                ].astype(F32)
            dst[c, pl.ds(r, step)] = total.astype(BF16)
            return 0

        lax.fori_loop(0, cut[k + 1] // step, body, 0)

    stages = [("s", k) for k in range(4)] + [("g", k) for k in (3, 2, 1, 0) if k < 3 or split]
    copies = {"s": scatter_copy, "g": gather_copy}

    def finish(c, n):
        kind, k = stages[n]
        for o in range(1, sizes[k]):
            copies[kind](c, k, o).wait_recv()
        if kind == "s":
            add(c, k)
        if n + 1 < len(stages):
            kind, k = stages[n + 1]
            for o in range(1, sizes[k]):
                copies[kind](c, k, o).start()

    last = LAG * (len(stages) - 1) + AHEAD

    def turn(t, _):
        for n in range(len(loads)):

            @pl.when(t == due[n])
            def _():
                loads[n].wait()

        @pl.when(t < chunks - 1)
        def _():
            left = l_ref[pick(t, left_at)]
            right = m_ref[pick(t, right_at)]
            w_ref[t] = outer(left, right).astype(BF16)
            ones = jnp.ones((16, T), BF16)
            t_ref[pl.ds(pick(t, right_at), 1)] = dot(ones, right)[:1]

        @pl.when(t == chunks - 1)
        def _():
            w_ref[chunks - 1, pl.ds(used, t_ref.shape[0])] = t_ref[...].astype(BF16)

        @pl.when((t >= 1) & (t <= chunks))
        def _():
            for o in range(1, sizes[0]):
                scatter_copy(t - 1, 0, o).start()

        for n in range(len(stages) - 1, -1, -1):
            c = t - AHEAD - LAG * n

            @pl.when((c >= 0) & (c < chunks))
            def _():
                finish(c, n)

        for c in range(chunks):

            @pl.when(t == c + last)
            def _():
                out_copy(c).start()

        return 0

    lax.fori_loop(0, chunks + last, turn, 0)

    def drain(c, _):
        for kind, k in stages:
            for o in range(1, sizes[k]):
                copies[kind](c, k, o).wait_send()
        return 0

    lax.fori_loop(0, chunks, drain, 0)
    move.wait()
    for c in range(chunks):
        out_copy(c).wait()


def sum_everywhere(products, short, used, pieces, F, sizes, cid):
    arrays, lefts, rights = [], [], []
    places, left_at, right_at, shapes = [], [], [], []

    def slots_of(pieces, slots):
        found = []
        for array, width in pieces:
            which = next((n for n, a in enumerate(arrays) if a is array), None)
            if which is None:
                which = len(arrays)
                arrays.append(array)
            for col in range(0, width, TILE):
                if (which, col) not in slots:
                    slots.append((which, col))
                found.append(slots.index((which, col)))
        return found

    for n, (left, right) in enumerate(products):
        a, b = slots_of(left, lefts), slots_of(right, rights)
        shapes.append((len(a) * TILE, len(b) * TILE))
        for i, u in enumerate(a):
            for j, v in enumerate(b):
                places.append((n, i * TILE, j * TILE))
                left_at.append(u)
                right_at.append(v)
    places.append((len(products), 0, 0))
    shapes.append(short.shape)
    T = min(a.shape[0] for a in arrays)
    chunks = len(places)
    cut = [TILE]
    for n in sizes:
        cut.append(cut[-1] // n)
    if cut[4] % 16:
        cut[4] = cut[3]
    most = max(sizes) - 1
    spec = pl.BlockSpec(memory_space=pl.ANY)
    sums = len(rights) + -len(rights) % 16
    plan = (places, left_at, right_at, lefts, rights, len(arrays) + 2, len(shapes) + 1)
    return pl.pallas_call(
        functools.partial(sum_kernel, sizes, F, used, plan),
        in_specs=[spec] * (len(arrays) + 2),
        out_specs=[spec] * (len(shapes) + 1),
        out_shape=[jax.ShapeDtypeStruct(v, BF16) for v in shapes]
        + [jax.ShapeDtypeStruct(pieces.shape, pieces.dtype)],
        scratch_shapes=[
            pltpu.VMEM((len(lefts), T, TILE), BF16),
            pltpu.VMEM((len(rights), T, TILE), BF16),
            pltpu.VMEM((sums, TILE), F32),
        ]
        + [pltpu.VMEM((chunks, TILE, TILE), BF16)] * 2
        + [pltpu.VMEM((chunks, sizes[k] - 1, cut[k + 1], TILE), BF16) for k in range(4)]
        + [
            pltpu.SemaphoreType.DMA((chunks, 8, most)),
            pltpu.SemaphoreType.DMA((chunks, 8, most)),
            pltpu.SemaphoreType.DMA((len(lefts) + len(rights) + 1,)),
            pltpu.SemaphoreType.DMA((chunks,)),
        ]
        + move_sems(pieces.shape[0]),
        compiler_params=pltpu.CompilerParams(
            collective_id=cid, has_side_effects=True, vmem_limit_bytes=60 << 20
        ),
    )(*arrays, short, pieces)


def on_device(
    mel_frames,
    window_count,
    stem_weight,
    stem_bias,
    reduce_weight,
    reduce_bias,
    first_gain,
    first_shift,
    query_weight,
    query_bias,
    key_weight,
    value_weight,
    value_bias,
    output_weight,
    output_bias,
    second_gain,
    second_shift,
    hidden_weight,
    hidden_bias,
    return_weight,
    return_bias,
    cotangent,
):
    S, piece_frames, mels = mel_frames.shape
    piece = cotangent.shape[1]
    D = stem_weight.shape[2]
    hd = D // HEADS
    scale = hd ** (-0.5)
    F = lax.axis_size("frame")
    G = F // S
    T = S * piece
    R = -(-(T + 2) // 128) * 128
    f = lax.axis_index("frame")
    s = f // G
    r = f % G
    alive = s < window_count[0]

    def gather_window(x):
        parts = []
        out = jnp.zeros((S * x.shape[1], x.shape[2]), x.dtype)
        for t in range(S):
            part = lax.dynamic_index_in_dim(x, (f + t) % S, 0, keepdims=False)
            perm = [(p, ((p % S + t) % S) * G + p // S) for p in range(F)]
            got = lax.ppermute(part, "frame", perm)
            j = (s - t) % S
            out = lax.dynamic_update_slice(out, got, (j * x.shape[1], 0))
        return out

    down = [(i, i + 1) for i in range(F) if (i + 1) % G != 0]
    up = [(i + 1, i) for i in range(F) if (i + 1) % G != 0]

    def with_halo(x):
        before = lax.ppermute(x[T - 1 : T], "frame", down)
        after = lax.ppermute(x[0:1], "frame", up)
        gap = jnp.zeros((R - T - 2, x.shape[1]), x.dtype)
        return jnp.concatenate([x, after, gap, before], axis=0)

    mel = gather_window(mel_frames.reshape(S, piece, 2 * mels))
    mel = with_halo(mel)
    odd_before = jnp.roll(mel[:, mels:], 1, axis=0)
    even_after = jnp.roll(mel[:, :mels], -1, axis=0)
    columns = jnp.concatenate([odd_before, mel, even_after], axis=1)
    stem_matrix = stem_weight.reshape(3 * mels, D)
    gap = jnp.zeros((mels, D), BF16)
    stem_pair = jnp.concatenate(
        [
            jnp.concatenate([stem_matrix, gap], axis=0),
            jnp.concatenate([gap, stem_matrix], axis=0),
        ],
        axis=1,
    )
    stem_bias2 = jnp.concatenate([stem_bias, stem_bias])
    stem_linear = dot(columns, stem_pair) + stem_bias2
    row = lax.broadcasted_iota(jnp.int32, (R, 1), 0)
    valid = (row < T) | ((row == T) & (r < G - 1)) | ((row == R - 1) & (r > 0))
    stem_active = jnp.where(valid, gelu(stem_linear), 0.0).astype(BF16)

    odd_active_before = jnp.roll(stem_active[:, D:], 1, axis=0)[:T]
    conv_columns = jnp.concatenate([odd_active_before, stem_active[:T]], axis=1)
    reduce_matrix = reduce_weight.reshape(3 * D, D)
    conv_linear = dot(conv_columns, reduce_matrix) + reduce_bias
    stream = gelu(conv_linear) + positions_of(r * T, T, D)
    xhat1, r1 = norm_parts(stream)
    first_normed = (xhat1 * first_gain + first_shift).astype(BF16)
    query = (dot(first_normed, query_weight) + query_bias).astype(BF16)
    key = dot(first_normed, key_weight).astype(BF16)
    value = (dot(first_normed, value_weight) + value_bias).astype(BF16)
    key = jnp.pad(key, ((0, -T % 16), (0, 0)))
    value = jnp.pad(value, ((0, -T % 16), (0, 0)))
    query_ext = jnp.pad(query, ((0, R - T), (0, 0)))
    block = 256 if R % 256 == 0 else 128
    probs, attended_wide, key_all, value_all, cot = attn_fwd(
        query_ext, key, value, cotangent, scale, HEADS, block, F, T
    )
    cot = cot.reshape(T, D)
    cot = jnp.where(alive, cot, jnp.zeros_like(cot))
    attended = attended_wide[:T].astype(BF16)
    mixed = stream + dot(attended, output_weight) + output_bias
    xhat2, r2 = norm_parts(mixed)
    second_normed = (xhat2 * second_gain + second_shift).astype(BF16)
    hidden_linear = dot(second_normed, hidden_weight) + hidden_bias
    hidden_cdf, hidden_pdf = phi_parts(hidden_linear)
    hidden_active = (hidden_linear * hidden_cdf).astype(BF16)
    layer = mixed + dot(hidden_active, return_weight) + return_bias
    layer = jnp.where(alive, layer, 0.0).astype(BF16)

    slope = hidden_cdf + hidden_linear * hidden_pdf
    hidden_grad = (slope * dot_t(cot, return_weight)).astype(BF16)
    inner, second_gain_grad, second_shift_grad = norm_pull(
        xhat2, r2, second_gain, dot_t(hidden_grad, hidden_weight)
    )
    mixed_grad = cot.astype(F32) + inner
    branch_grad = mixed_grad.astype(BF16)

    attended_grad = jnp.pad(dot_t(branch_grad, output_weight).astype(BF16), ((0, R - T), (0, 0)))
    query_wide, key_grad, value_grad, layer_output = attn_bwd(
        query_ext,
        attended_grad,
        attended_wide,
        key_all,
        value_all,
        probs,
        layer.reshape(S, piece, D),
        scale,
        HEADS,
        block,
        F,
    )
    query_grad, key_grad, value_grad = query_wide[:T], key_grad[:T], value_grad[:T]
    normed_grad = (
        dot_t(query_grad, query_weight)
        + dot_t(key_grad, key_weight)
        + dot_t(value_grad, value_weight)
    )
    inner, first_gain_grad, first_shift_grad = norm_pull(xhat1, r1, first_gain, normed_grad)
    stream_grad = mixed_grad + inner
    conv_grad = (gelu_slope(conv_linear) * stream_grad).astype(BF16)
    conv_ext = with_halo(conv_grad)
    conv_after = jnp.roll(conv_ext, -1, axis=0)
    pair_grad = dot_t(conv_ext, reduce_matrix[D:])
    third_grad = dot_t(conv_after, reduce_matrix[:D])
    active_grad = pair_grad + jnp.concatenate([jnp.zeros_like(third_grad), third_grad], axis=1)
    stem_grad = jnp.where(valid, gelu_slope(stem_linear) * active_grad, 0.0).astype(BF16)
    own = stem_grad[:T]
    totals = column_total(own)
    stem_bias_grad = totals[:D] + totals[D:]
    pair_matrix_grad = outer(columns[:T], own)
    stem_matrix_grad = pair_matrix_grad[: 3 * mels, :D] + pair_matrix_grad[mels:, D:]
    mel_columns = dot_t(stem_grad, stem_pair)
    mel_pair = (
        mel_columns[:, mels : 3 * mels]
        + jnp.concatenate(
            [
                jnp.roll(mel_columns[:, 3 * mels :], 1, axis=0),
                jnp.roll(mel_columns[:, :mels], -1, axis=0),
            ],
            axis=1,
        )
    )[:T]
    sizes = (2, F // 2, F // 2, lax.axis_size("dp") // (F // 2))
    small = [stem_bias_grad, first_gain_grad, first_shift_grad, second_gain_grad, second_shift_grad]
    at = 3 * mels
    used = at + len(small) + -(at + len(small)) % 16
    short = jnp.pad(stem_matrix_grad, ((0, TILE - at), (0, 0)))
    place = lax.broadcasted_iota(jnp.int32, (TILE, 1), 0)
    for n, v in enumerate(small):
        short = jnp.where(place == at + n, v[None, :], short)
    FF = hidden_weight.shape[1]
    one = [(first_normed, D)]
    *terms, mel_slots = sum_everywhere(
        [
            ([(hidden_active, FF)], [(cot, D)]),
            ([(second_normed, D)], [(hidden_grad, FF)]),
            ([(attended, D)], [(branch_grad, D)]),
            ([(odd_active_before, D), (stem_active, 2 * D)], [(conv_grad, D)]),
            (one, [(query_wide, D)]),
            (one, [(key_grad, D)]),
            (one, [(value_grad, D)]),
        ],
        short.astype(BF16),
        used,
        mel_pair.reshape(S, piece, 2 * mels),
        F,
        sizes,
        0,
    )
    mel_gradient = mel_slots.reshape(S, piece_frames, mels)
    return_w, hidden_w, output_w, reduce_w, query_w, key_w, value_w, short = [
        v.astype(F32) for v in terms
    ]
    stem_w = short[: 3 * mels]
    small = [short[at + n] for n in range(len(small))]
    sums = short[used:]
    wide = FF // D
    return (
        layer_output,
        mel_gradient,
        stem_w.reshape(3, mels, D),
        small[0],
        reduce_w.reshape(3, D, D),
        sums[wide + 2],
        small[1],
        small[2],
        query_w,
        sums[wide + 3],
        key_w,
        value_w,
        sums[wide + 5],
        output_w,
        sums[wide + 1],
        small[3],
        small[4],
        hidden_w,
        sums[1 : wide + 1].reshape(FF),
        return_w,
        sums[0],
    )


def solution(mesh):
    cut = P("dp", "frame", None)
    return jax.shard_map(
        on_device,
        mesh=mesh,
        in_specs=(cut, P("dp")) + (P(),) * 19 + (cut,),
        out_specs=(cut, cut) + (P(),) * 19,
        check_vma=False,
    )
```

profile of v0, /device:TPU:0, one launch (start us, length us, event | category | flops | bytes accessed | tf_op | source)
XLA Modules:
  0.0 256.5 jit_solution(14302374743241233181)
XLA Ops:
  0.7 1.3 copy.45
  3.0 4.2 %collective-permute-start.1 = (bf16[376,160]{1,0:T(8,128)(2,1)S(1)}, bf16[376,160]{1,0:T(8,128)(2,1)S(1)}, u32[]{:S(2)}, u32[]{:S(2)}) collective-permute-start(bf16[376,160]{1,0:T(8,128)(2,1)S(1)} %get-tuple-element.129), channel_id=1, source_target_pairs={{0,2},{1,0},{2,3},{3,1},{4,6},{5,4},{6,7},{7,5},{8,10},{9,8},{10,1... | collective-permute-start | bytes 360968 | tf_op jit(solution)/shard_map/ppermute | solution.py:778
  7.7 1.4 multiply_add_fusion.10
  9.2 2.6 %collective-permute-done.1 = bf16[376,160]{1,0:T(8,128)(2,1)S(1)} collective-permute-done((bf16[376,160]{1,0:T(8,128)(2,1)S(1)}, bf16[376,160]{1,0:T(8,128)(2,1)S(1)}, u32[]{:S(2)}, u32[]{:S(2)}) %collective-permute-start.1) | collective-permute-done | bytes 120352 | tf_op jit(solution)/shard_map/ppermute | solution.py:778
  11.8 2.8 %collective-permute-start.2 = (bf16[1,160]{1,0:T(2,128)(2,1)S(1)}, bf16[1,160]{1,0:T(2,128)(2,1)S(1)}, u32[]{:S(2)}, u32[]{:S(2)}) collective-permute-start(bf16[1,160]{1,0:T(2,128)(2,1)S(1)} %get-tuple-element.128), channel_id=1, source_target_pairs={{0,1},{2,3},{4,5},{6,7},{8,9},{10,11},{12,13},{14,15},{16,17},{18,... | collective-permute-start | bytes 968 | tf_op jit(solution)/shard_map/ppermute | solution.py:787
  14.6 1.3 collective-permute-start.3
  16.6 1.0 collective-permute-done.3
  17.7 6.2 %select_convert_fusion.1 = (bf16[768,1024]{1,0:T(8,128)(2,1)S(1)}, f32[768,1024]{1,0:T(8,128)}) fusion(f32[1024]{0:T(1024)S(1)} %pad_maximum_fusion.12, pred[768]{0:T(1024)(128)(4,1)S(1)} %fusion.71, bf16[240,512]{1,0:T(8,128)(2,1)} %bitcast.81, bf16[1,160]{1,0:T(2,128)(2,1)S(1)} %collective-permute-done.2, bf16[14,160]{1,0:T(8,128)(2,1)S(1)} %broadcast_in_dim.121, ...), kind=kOutput, calls=%fused_computation.13 | convolution fusion | flops 531988480 | bytes 5215296 | tf_op jit(solution)/shard_map/dot_general | solution.py:49
  24.1 0.9 copy-done.2
  25.8 0.8 copy-done.22
  26.6 3.8 %fusion.84 = (f32[752]{0:T(1024)S(1)}, f32[752,512]{1,0:T(8,128)S(1)}, f32[752,512]{1,0:T(8,128)}) fusion(f32[752,256]{1,0:T(8,128)S(1)} %bitcast.66, f32[752,256]{1,0:T(8,128)S(1)} %bitcast.65, f32[512]{0:T(512)S(1)} %copy-done.44, bf16[1536,512]{1,0:T(8,128)(2,1)S(1)} %bitcast.68, bf16[752,1024]{1,0:T(8,128)(2,1)S(1)} %slice.218, ...), kind=kOutput, calls=%fused_computation.171 | convolution fusion | flops 1197423872 | bytes 8508352 | tf_op jit(solution)/shard_map/dot_general | solution.py:49
  32.4 0.9 pad.14.q_ref
  33.3 1.4 convolution_convert_fusion.1.k_own
  34.8 1.4 add_convert_fusion.1.v_own
  36.2 27.3 %shard_map.373 = (bf16[8,1504,768]{2,1,0:T(8,128)(2,1)}, f32[768,512]{1,0:T(8,128)}, bf16[1504,512]{1,0:T(8,128)(2,1)}, bf16[1504,512]{1,0:T(8,128)(2,1)}, bf16[2,376,512]{2,1,0:T(8,128)(2,1)}) custom-call(bf16[768,512]{1,0:T(8,128)(2,1)} %pad.14.q_ref, bf16[752,512]{1,0:T(8,128)(2,1)} %convolution_convert_fusion.1.k_own, ...), custom_call_target="tpu_custom_call" | custom-call | tf_op jit(solution)/shard_map/pallas_call | solution.py:291
  63.5 2.2 fusion.90
  66.1 0.7 copy-done.21
  67.7 6.8 %multiply_convert_fusion = (bf16[752,2048]{1,0:T(8,128)(2,1)S(1)}, f32[752,2048]{1,0:T(8,128)S(1)}) fusion(f32[2048]{0:T(1024)S(1)} %copy-done.43, bf16[752,512]{1,0:T(8,128)(2,1)S(1)} %add_convert_fusion.refs_2_, bf16[512,2048]{1,0:T(8,128)(2,1)S(1)} %copy-done), kind=kOutput, calls=%fused_computation.3 | convolution fusion | flops 1614020608 | bytes 12115968 | tf_op jit(solution)/shard_map/dot_general | solution.py:49
  74.5 7.2 %multiply_convert_fusion.1.refs_3_ = bf16[752,2048]{1,0:T(8,128)(2,1)S(1)} fusion(f32[752,2048]{1,0:T(8,128)S(1)} %get-tuple-element.144, bf16[752,512]{1,0:T(8,128)(2,1)S(1)} %bitcast.60, bf16[2048,512]{1,0:T(8,128)(2,1)S(1)} %copy-done.41, f32[2048]{0:T(1024)S(1)} %copy-done.43), kind=kOutput, calls=%fused_computation.4 | convolution fusion | flops 1618640896 | bytes 12115968 | tf_op jit(solution)/shard_map/dot_general | solution.py:53
  81.7 2.2 multiply_reduce_fusion.1
  84.0 1.8 fusion.83
  86.3 0.9 pad.15.do_ref
  87.3 2.7 %select_convert_fusion.2 = bf16[752,512]{1,0:T(8,128)(2,1)} fusion(f32[752,512]{1,0:T(8,128)S(1)} %get-tuple-element.141, bf16[752,2048]{1,0:T(8,128)(2,1)S(1)} %get-tuple-element.143.refs_0_, bf16[2048,512]{1,0:T(8,128)(2,1)S(1)} %copy-done.41, f32[512]{0:T(512)S(1)} %copy-done.47, pred[]{:T(512)S(6)} %lt.57), kind=kOutput, calls=%fused_computation.33 | convolution fusion | flops 1578598400 | bytes 7489537 | tf_op jit(solution)/shard_map/dot_general | solution.py:49
  89.9 29.1 %shard_map.374 = (bf16[768,512]{1,0:T(8,128)(2,1)}, bf16[752,512]{1,0:T(8,128)(2,1)}, bf16[752,512]{1,0:T(8,128)(2,1)}, bf16[2,376,512]{2,1,0:T(8,128)(2,1)}) custom-call(bf16[768,512]{1,0:T(8,128)(2,1)} %pad.14.q_ref, bf16[768,512]{1,0:T(8,128)(2,1)} %pad.15.do_ref, f32[768,512]{1,0:T(8,128)} %get-tuple-element.40.o_ref, ...), custom_call_target="tpu_custom_call" | custom-call | tf_op jit(solution)/shard_map/pallas_call | solution.py:443
  119.1 1.8 fusion.18
  122.2 1.2 multiply_reduce_fusion
  124.1 2.0 multiply_convert_fusion.2.refs_8_
  126.1 2.3 collective-permute-start.5
  128.4 1.3 collective-permute-start.4
  129.9 2.4 slice.260.refs_4_
  133.3 1.1 copy-done.48
  134.4 4.7 %select_convert_fusion = bf16[768,1024]{1,0:T(8,128)(2,1)S(1)} fusion(f32[768,512]{1,0:T(8,128)S(1)} %fusion.14, f32[768,1024]{1,0:T(8,128)S(1)} %copy-done.48, bf16[1024,512]{1,0:T(8,128)(2,1)S(1)} %bitcast.64, f32[1024]{0:T(1024)S(1)} %pad_maximum_fusion.12, pred[768]{0:T(1024)(128)(4,1)S(1)} %fusion.71, bf16[1,512]{1,0:T(2,128)(2,1)S(1)} %collective-permute-done.5, ...), kind=kOutput, calls=%fused_computation.12 | convolution fusion | flops 831258624 | bytes 8118528 | tf_op jit(solution)/shard_map/dot_general | solution.py:53
  141.0 1.3 fusion.10
  142.6 1.1 copy.46
  143.8 1.4 select_convert_fusion.3.refs_13_
  145.2 90.9 %shard_map.375 = (bf16[2048,512]{1,0:T(8,128)(2,1)}, bf16[512,2048]{1,0:T(8,128)(2,1)}, bf16[512,512]{1,0:T(8,128)(2,1)}, bf16[1536,512]{1,0:T(8,128)(2,1)}, bf1...) custom-call(bf16[752,2048]{1,0:T(8,128)(2,1)} %copy-done.6, ...), custom_call_target="tpu_custom_call" | custom-call | tf_op jit(solution)/shard_map/pallas_call | solution.py:708
  236.1 1.9 slice.232
  237.9 1.5 fusion.88
  239.4 1.2 convert_element_type.114
  240.8 1.0 copy.47
  241.9 3.6 %convert.5 = f32[3,512,512]{2,1,0:T(8,128)} convert(bf16[3,512,512]{2,1,0:T(8,128)(2,1)} %bitcast.63) | non-fusion elementwise | flops 786432 | bytes 4718592 | tf_op jit(solution)/shard_map/reshape | solution.py:934
  245.4 1.1 convert_element_type.115
  246.5 1.1 convert_element_type.116
  247.7 1.1 convert_element_type.117
  248.8 1.1 convert_element_type.118
  249.9 2.5 convert_element_type.119
  253.0 2.6 %convert_element_type.120 = f32[2048,512]{1,0:T(8,128)} convert(bf16[2048,512]{1,0:T(8,128)(2,1)S(1)} %copy-done.14) | non-fusion elementwise | flops 1048576 | bytes 6291456 | tf_op jit(solution)/shard_map/convert_element_type | solution.py:923
  255.6 0.9 copy.53
  (155 shorter events, 12.2 us)
Async XLA Ops:
  0.7 66.6 %copy-start = (bf16[512,2048]{1,0:T(8,128)(2,1)S(1)}, bf16[512,2048]{1,0:T(8,128)(2,1)}, u32[]{:S(2)}) copy-start(bf16[512,2048]{1,0:T(8,128)(2,1)} %param.39) | copy-start | bytes 6291460
  0.7 7.0 %copy-start.40 = (f32[512]{0:T(512)S(1)}, f32[512]{0:T(512)}, u32[]{:S(2)}) copy-start(f32[512]{0:T(512)} %param.25) | copy-start | bytes 6148
  2.3 6.8 %collective-permute-start = (bf16[376,160]{1,0:T(8,128)(2,1)S(1)}, bf16[376,160]{1,0:T(8,128)(2,1)S(1)}, u32[]{:S(2)}, u32[]{:S(2)}) collective-permute-start(bf16[376,160]{1,0:T(8,128)(2,1)S(1)} %get-tuple-element.130), channel_id=1, source_target_pairs={{0,0},{1,2},{2,1},{3,3},{4,4},{5,6},{6,5},{7,7},{8,8},{9,10},{10,9... | collective-permute-start | bytes 360968 | tf_op jit(solution)/shard_map/ppermute | solution.py:778
  3.0 8.8 %collective-permute-start.1 = (bf16[376,160]{1,0:T(8,128)(2,1)S(1)}, bf16[376,160]{1,0:T(8,128)(2,1)S(1)}, u32[]{:S(2)}, u32[]{:S(2)}) collective-permute-start(bf16[376,160]{1,0:T(8,128)(2,1)S(1)} %get-tuple-element.129), channel_id=1, source_target_pairs={{0,2},{1,0},{2,3},{3,1},{4,6},{5,4},{6,7},{7,5},{8,10},{9,8},{10,1... | collective-permute-start | bytes 360968 | tf_op jit(solution)/shard_map/ppermute | solution.py:778
  11.8 4.7 %collective-permute-start.2 = (bf16[1,160]{1,0:T(2,128)(2,1)S(1)}, bf16[1,160]{1,0:T(2,128)(2,1)S(1)}, u32[]{:S(2)}, u32[]{:S(2)}) collective-permute-start(bf16[1,160]{1,0:T(2,128)(2,1)S(1)} %get-tuple-element.128), channel_id=1, source_target_pairs={{0,1},{2,3},{4,5},{6,7},{8,9},{10,11},{12,13},{14,15},{16,17},{18,... | collective-permute-start | bytes 968 | tf_op jit(solution)/shard_map/ppermute | solution.py:787
  14.6 3.1 %collective-permute-start.3 = (bf16[1,160]{1,0:T(2,128)(2,1)S(1)}, bf16[1,160]{1,0:T(2,128)(2,1)S(1)}, u32[]{:S(2)}, u32[]{:S(2)}) collective-permute-start(bf16[1,160]{1,0:T(2,128)(2,1)S(1)} %get-tuple-element.127), channel_id=1, source_target_pairs={{1,0},{3,2},{5,4},{7,6},{9,8},{11,10},{13,12},{15,14},{17,16},{19,... | collective-permute-start | bytes 968 | tf_op jit(solution)/shard_map/ppermute | solution.py:788
  23.9 1.2 copy-start.2
  24.0 1.6 copy-start.18
  24.0 1.8 copy-start.19
  24.0 2.6 %copy-start.22 = (bf16[3,512,512]{2,1,0:T(8,128)(2,1)S(1)}, bf16[3,512,512]{2,1,0:T(8,128)(2,1)}, u32[]{:S(2)}) copy-start(bf16[3,512,512]{2,1,0:T(8,128)(2,1)} %param.26) | copy-start | bytes 4718596
  24.0 2.6 %copy-start.44 = (f32[512]{0:T(512)S(1)}, f32[512]{0:T(512)}, u32[]{:S(2)}) copy-start(f32[512]{0:T(512)} %param.27) | copy-start | bytes 6148
  25.2 5.2 %copy-start.12 = (bf16[752,512]{1,0:T(8,128)(2,1)}, bf16[752,512]{1,0:T(8,128)(2,1)S(1)}, u32[]{:S(2)}) copy-start(bf16[752,512]{1,0:T(8,128)(2,1)S(1)} %pad_maximum_fusion.1.refs_6_) | copy-start | bytes 2310148
  31.8 3.0 %copy-start.8 = (bf16[752,512]{1,0:T(8,128)(2,1)}, bf16[752,512]{1,0:T(8,128)(2,1)S(1)}, u32[]{:S(2)}) copy-start(bf16[752,512]{1,0:T(8,128)(2,1)S(1)} %add_convert_fusion.3.refs_9_) | copy-start | bytes 2310148
  31.8 1.5 copy-start.32
  32.4 2.4 copy-start.24
  32.4 2.4 copy-start.46
  36.2 27.3 %copy-start.38 = (f32[512]{0:T(512)S(1)}, f32[512]{0:T(512)}, u32[]{:S(2)}) copy-start(f32[512]{0:T(512)} %param.36) | copy-start | bytes 6148
  65.7 1.1 copy-start.21
  65.7 1.2 copy-start.36
  65.7 1.2 copy-start.39
  66.9 17.0 %copy-start.4 = (bf16[2,376,512]{2,1,0:T(8,128)(2,1)}, bf16[2,376,512]{2,1,0:T(8,128)(2,1)S(1)}, u32[]{:S(2)}) copy-start(bf16[2,376,512]{2,1,0:T(8,128)(2,1)S(1)} %broadcast_select_fusion) | copy-start | bytes 2310148
  67.7 6.8 %copy-start.9 = (bf16[752,512]{1,0:T(8,128)(2,1)}, bf16[752,512]{1,0:T(8,128)(2,1)S(1)}, u32[]{:S(2)}) copy-start(bf16[752,512]{1,0:T(8,128)(2,1)S(1)} %add_convert_fusion.refs_2_) | copy-start | bytes 2310148
  67.7 6.8 %copy-start.41 = (bf16[2048,512]{1,0:T(8,128)(2,1)S(1)}, bf16[2048,512]{1,0:T(8,128)(2,1)}, u32[]{:S(2)}) copy-start(bf16[2048,512]{1,0:T(8,128)(2,1)} %param.41) | copy-start | bytes 6291460
  74.5 12.8 %copy-start.6 = (bf16[752,2048]{1,0:T(8,128)(2,1)}, bf16[752,2048]{1,0:T(8,128)(2,1)S(1)}, u32[]{:S(2)}) copy-start(bf16[752,2048]{1,0:T(8,128)(2,1)S(1)} %get-tuple-element.143.refs_0_) | copy-start | bytes 9240580
  81.7 2.2 copy-start.7
  84.0 1.8 copy-start.34
  85.7 1.5 copy-start.13
  85.7 1.5 copy-start.47
  89.9 29.2 %copy-start.31 = (bf16[512,512]{1,0:T(8,128)(2,1)S(1)}, bf16[512,512]{1,0:T(8,128)(2,1)}, u32[]{:S(2)}) copy-start(bf16[512,512]{1,0:T(8,128)(2,1)} %param.30) | copy-start | bytes 1572868
  119.1 1.9 copy-start.10
  119.1 1.9 copy-start.33
  120.9 1.1 copy-start.11
  121.0 1.3 copy-start.25
  122.2 1.4 copy-start.5
  122.2 1.9 copy-start.16
  124.1 5.6 %copy-start.23 = (bf16[3,512,512]{2,1,0:T(8,128)(2,1)S(1)}, bf16[3,512,512]{2,1,0:T(8,128)(2,1)}, u32[]{:S(2)}) copy-start(bf16[3,512,512]{2,1,0:T(8,128)(2,1)} %param.26) | copy-start | bytes 4718596
  126.1 7.2 %copy-start.3 = (bf16[752,512]{1,0:T(8,128)(2,1)}, bf16[752,512]{1,0:T(8,128)(2,1)S(1)}, u32[]{:S(2)}) copy-start(bf16[752,512]{1,0:T(8,128)(2,1)S(1)} %multiply_convert_fusion.2.refs_8_) | copy-start | bytes 2310148
  126.1 6.1 %collective-permute-start.5 = (bf16[1,512]{1,0:T(2,128)(2,1)S(1)}, bf16[1,512]{1,0:T(2,128)(2,1)S(1)}, u32[]{:S(2)}, u32[]{:S(2)}) collective-permute-start(bf16[1,512]{1,0:T(2,128)(2,1)S(1)} %get-tuple-element.115), channel_id=1, source_target_pairs={{0,1},{2,3},{4,5},{6,7},{8,9},{10,11},{12,13},{14,15},{16,17},{18,... | collective-permute-start | bytes 3080 | tf_op jit(solution)/shard_map/ppermute | solution.py:787
  128.4 3.9 %collective-permute-start.4 = (bf16[1,512]{1,0:T(2,128)(2,1)S(1)}, bf16[1,512]{1,0:T(2,128)(2,1)S(1)}, u32[]{:S(2)}, u32[]{:S(2)}) collective-permute-start(bf16[1,512]{1,0:T(2,128)(2,1)S(1)} %get-tuple-element.116), channel_id=1, source_target_pairs={{1,0},{3,2},{5,4},{7,6},{9,8},{11,10},{13,12},{15,14},{17,16},{19,... | collective-permute-start | bytes 3080 | tf_op jit(solution)/shard_map/ppermute | solution.py:788
  132.5 1.9 copy-start.48
  236.0 4.6 %copy-start.20 = (f32[2,376,160]{2,1,0:T(8,128)S(1)}, f32[2,376,160]{2,1,0:T(8,128)}, u32[]{:S(2)}) copy-start(f32[2,376,160]{2,1,0:T(8,128)} %get-tuple-element.48) | copy-start | bytes 1443844
  241.9 3.6 %copy-start.29 = (bf16[512,512]{1,0:T(8,128)(2,1)S(1)}, bf16[512,512]{1,0:T(8,128)(2,1)}, u32[]{:S(2)}) copy-start(bf16[512,512]{1,0:T(8,128)(2,1)} %get-tuple-element.51) | copy-start | bytes 1572868
  245.4 2.2 copy-start.27
  246.5 2.2 copy-start.26
  247.6 2.2 copy-start.15
  249.9 3.2 %copy-start.14 = (bf16[2048,512]{1,0:T(8,128)(2,1)S(1)}, bf16[2048,512]{1,0:T(8,128)(2,1)}, u32[]{:S(2)}) copy-start(bf16[2048,512]{1,0:T(8,128)(2,1)} %get-tuple-element.56) | copy-start | bytes 6291460
  253.0 2.6 %copy-start.17 = (bf16[2,376,512]{2,1,0:T(8,128)(2,1)S(1)}, bf16[2,376,512]{2,1,0:T(8,128)(2,1)}, u32[]{:S(2)}) copy-start(bf16[2,376,512]{2,1,0:T(8,128)(2,1)} %get-tuple-element.173) | copy-start | bytes 2310148
  253.0 3.5 %copy-start.1 = (bf16[512,2048]{1,0:T(8,128)(2,1)S(1)}, bf16[512,2048]{1,0:T(8,128)(2,1)}, u32[]{:S(2)}) copy-start(bf16[512,2048]{1,0:T(8,128)(2,1)} %param.39) | copy-start | bytes 6291460
  (7 other events, 6.2 us)
where the time goes:
time: 258 us; the launch traced here: 257 us
  Pallas kernels  147 us (57%)
  matrix products  46.1 us (18%)
  other arithmetic  23.5 us (9%)
  local copies, waits for them, and re-layouts  21.3 us (8%)
  starting transfers between devices  12.5 us (5%)
  waiting for transfers between devices  3.62 us (1%)
    pallas_call x1, Pallas kernels, sum_everywhere(): pl.pallas_call(functools.partial(sum_kernel, sizes, F, used, plan), in_sp...  90.9 us
    pallas_call x1, Pallas kernels, attn_bwd(): pl.pallas_call(functools.partial(bwd_kernel, scale, hd, F, G, pairs), gri...  29.1 us
    pallas_call x1, Pallas kernels, attn_fwd(): pl.pallas_call(functools.partial(fwd_kernel, scale, hd, F, G, T, pairs),...  27.3 us
    dot_general x8, matrix products, dot(): return jnp.dot(left, right, preferred_element_type=F32)  25.1 us
    dot_general x9, matrix products, dot_t(): lax.dot_general(left, right, (((1,), (1,)), ((), ())), preferred_element_...  19.7 us
    unnamed x103, local copies, waits for them, and re-layouts  11.1 us
    convert_element_type x7, other arithmetic, on_device(): v.astype(F32)  10.7 us
  transfers between devices with their start and end apart: 6, of which 2 were waited for; matrix products, arithmetic and copies ran while one was open for 2% of the time, Pallas kernels for 0%

commit v1 on v0

--- a/solution.py
+++ b/solution.py
@@ -479,17 +479,196 @@
     return out
 
 
+class Rest:
+    FIRST = 2
+
+    def __init__(self, G, T, taps, m_ref, t_ref, w_ref, data, scratch, sems):
+        self.m, self.t, self.w = m_ref, t_ref, w_ref
+        self.data = data
+        self.ext, self.edge, self.halo, self.sg, self.y0, self.y1, self.y2 = scratch
+        self.send, self.recv = sems
+        self.G, self.T, self.taps = G, T, taps
+        self.R = self.sg.shape[0]
+        self.row = lax.rem(lax.axis_index("frame"), G)
+        self.size = 256 if self.R % 256 == 0 else 128
+        self.token_blocks = [(a, min(a + 256, T)) for a in range(0, T, 256)]
+        self.edges_at = self.FIRST + len(self.token_blocks)
+        self.halo_at = self.edges_at + 2
+        self.stem_at = self.halo_at + 1
+        self.mel_at = self.stem_at + self.R // self.size
+        self.weights_at = self.mel_at + 1
+        self.halo[...] = jnp.zeros_like(self.halo)
+
+    def due(self, name):
+        if name in ("reduce", "stem_linear", "stem_taps"):
+            return self.stem_at
+        if name in ("columns", "second"):
+            return self.weights_at
+        return self.FIRST
+
+    def tokens(self, n):
+        a, b = self.token_blocks[n]
+        q, k, v, conv, base = self.taps
+        data, rows = self.data, pl.ds(a, b - a)
+        dy = (
+            dot_t(self.m[q, rows], data["query"][...])
+            + dot_t(self.m[k, rows], data["key"][...])
+            + dot_t(self.m[v, rows], data["value"][...])
+        )
+        xhat = data["xhat"][rows]
+        r = data["r"][rows][:, :1]
+        dh = dy * data["gain"][...][:1]
+        inner = r * (
+            dh
+            - jnp.mean(dh, axis=-1, keepdims=True)
+            - xhat * jnp.mean(dh * xhat, axis=-1, keepdims=True)
+        )
+        self.t[base + 1 : base + 2] += jnp.sum(dy * xhat, axis=0, keepdims=True)
+        self.t[base + 2 : base + 3] += jnp.sum(dy, axis=0, keepdims=True)
+        grad = gelu_slope(data["conv_linear"][rows]) * (data["mixed"][rows] + inner)
+        grad = grad.astype(BF16)
+        self.m[conv, rows] = grad
+        self.ext[rows] = grad
+        if n == 0:
+            self.edge[1] = grad[:16]
+            self.ext[pl.ds(self.R, 16)] = grad[:16]
+        if b == self.T:
+            self.edge[0] = grad[b - a - 16 :]
+
+    def edge_copy(self, n):
+        return pltpu.make_async_remote_copy(
+            src_ref=self.edge.at[n],
+            dst_ref=self.halo.at[n],
+            send_sem=self.send.at[n],
+            recv_sem=self.recv.at[n],
+            device_id=group_peer(self.G, 1 if n == 0 else self.G - 1),
+            device_id_type=MESH,
+        )
+
+    def has(self, n):
+        return self.row < self.G - 1 if n == 0 else self.row > 0
+
+    def send_edges(self):
+        for n in range(2):
+
+            @pl.when(self.has(n))
+            def _():
+                self.edge_copy(n).start()
+
+    def fill_halo(self):
+        for n in range(2):
+
+            @pl.when(self.has(1 - n))
+            def _():
+                landed = self.halo.at[n]
+                pltpu.make_async_copy(landed, landed, self.recv.at[n]).wait()
+
+        at = self.T // 16 * 16
+        rows = pl.ds(at, self.R - at)
+        own = self.ext[rows].astype(F32)
+        place = lax.broadcasted_iota(jnp.int32, own.shape, 0) + at
+        before = self.halo[0].astype(F32)[15:16]
+        after = self.halo[1].astype(F32)[:1]
+        own = jnp.where(place < self.T, own, 0.0)
+        own = jnp.where(place == self.T, after, own)
+        own = jnp.where(place == self.R - 1, before, own)
+        self.ext[rows] = own.astype(BF16)
+
+    def stem(self, n):
+        data, a = self.data, n * self.size
+        D = self.ext.shape[1]
+        rows = pl.ds(a, self.size)
+        pair = dot_t(self.ext[rows], data["reduce"][pl.ds(D, 2 * D)])
+        third = dot_t(self.ext[pl.ds(a, self.size + 16)], data["reduce"][pl.ds(0, D)])
+        third = third[1 : self.size + 1]
+        active = jnp.concatenate([pair[:, :D], pair[:, D:] + third], axis=1)
+        place = lax.broadcasted_iota(jnp.int32, active.shape, 0) + a
+        high = self.T + jnp.where(self.row < self.G - 1, 1, 0)
+        low = self.R - jnp.where(self.row > 0, 1, 0)
+        grad = gelu_slope(data["stem_linear"][rows]) * active
+        grad = jnp.where((place < high) | (place >= low), grad, 0.0).astype(BF16)
+        self.sg[rows] = grad
+        self.y0[rows] = dot_t(grad, data["stem_taps"][0])
+        y1 = dot_t(grad, data["stem_taps"][1])
+        self.y1[pl.ds(a + 8, self.size)] = y1
+        if a + self.size == self.R:
+            self.y1[pl.ds(0, 8)] = y1[self.size - 8 :]
+        self.y2[rows] = dot_t(grad, data["stem_taps"][2])
+
+    def mel(self, out):
+        T = self.T
+        total = self.y0[pl.ds(0, T)] + self.y1[pl.ds(7, T)] + self.y2[pl.ds(1, T)]
+        n = out.shape[1]
+        for j in range(out.shape[0]):
+            out[j] = total[j * n : (j + 1) * n]
+
+    def weights(self):
+        base = self.taps[-1]
+        D = self.ext.shape[1]
+        own = self.sg[pl.ds(0, self.T)]
+        wide = outer(self.data["columns"][pl.ds(0, self.T)], own)
+        mels = wide.shape[0] // 4
+        sums = dot(jnp.ones((16, self.T), BF16), own)[:1]
+        self.w[self.w.shape[0] - 1, pl.ds(0, 3 * mels)] = (
+            wide[: 3 * mels, :D] + wide[mels:, D:]
+        ).astype(BF16)
+        self.t[base : base + 1] = sums[:, :D] + sums[:, D:]
+        self.t[base + 3 : base + 5] = self.data["second"][...][:2]
+
+    def step(self, t, out):
+        todo = [(self.FIRST + n, functools.partial(self.tokens, n)) for n in range(len(self.token_blocks))]
+        todo.append((self.edges_at, self.send_edges))
+        todo.append((self.halo_at, self.fill_halo))
+        todo += [
+            (self.stem_at + n, functools.partial(self.stem, n)) for n in range(self.R // self.size)
+        ]
+        todo.append((self.mel_at, functools.partial(self.mel, out)))
+        todo.append((self.weights_at, self.weights))
+        for at, work in todo:
+            pl.when(t == at)(work)
+
+    def drain(self):
+        for n in range(2):
+
+            @pl.when(self.has(n))
+            def _():
+                self.edge_copy(n).wait_send()
+
+
+REST = (
+    "query",
+    "key",
+    "value",
+    "xhat",
+    "r",
+    "gain",
+    "mixed",
+    "conv_linear",
+    "reduce",
+    "stem_linear",
+    "stem_taps",
+    "columns",
+    "second",
+)
+
+
 def sum_kernel(sizes, F, used, plan, *refs):
-    places, left_at, right_at, lefts, rights, n_in, n_out = plan
-    in_refs, short_ref, piece_ref = refs[: n_in - 2], refs[n_in - 2], refs[n_in - 1]
+    places, left_at, right_at, lefts, rights, n_in, n_out, taps, T = plan
+    extra = len(REST)
+    in_refs, rest_refs = refs[: n_in - extra], refs[n_in - extra : n_in]
     g_refs, slot_ref = refs[n_in : n_in + n_out - 1], refs[n_in + n_out - 1]
     refs = refs[n_in + n_out :]
     l_ref, m_ref, t_ref, w_ref, s_ref, r0, r1, r2, r3 = refs[:9]
-    send_sem, recv_sem, load_sem, out_sem, *sems = refs[9:]
+    kept, work = refs[9 : 9 + extra], refs[9 + extra : 16 + extra]
+    piece_ref, send_sem, recv_sem, load_sem, out_sem, edge_send, edge_recv, *sems = refs[16 + extra :]
     t_ref[...] = jnp.zeros_like(t_ref)
+    w_ref[len(places) - 1] = jnp.zeros(w_ref.shape[1:], BF16)
+    G = F // slot_ref.shape[0]
+    rest = Rest(
+        G, T, taps, m_ref, t_ref, w_ref, dict(zip(REST, kept)), work, (edge_send, edge_recv)
+    )
     recv = (r0, r1, r2, r3)
     chunks = len(places)
-    T = l_ref.shape[1]
     Y = sizes[2]
     dp = lax.axis_index("dp")
     fr = lax.axis_index("frame")
@@ -500,20 +679,18 @@
     first = core == 0
     me = (core, jnp.where(first, x, y), jnp.where(first, y, x), z)
 
-    loads = []
-    for buf, sources, base in ((l_ref, lefts, 0), (m_ref, rights, len(lefts))):
+    loads, due = [], []
+    for buf, sources, at in ((l_ref, lefts, left_at), (m_ref, rights, right_at)):
         for n, (which, col) in enumerate(sources):
+            if which is None:
+                continue
             src = in_refs[which].at[pl.ds(0, T), pl.ds(col, TILE)]
-            loads.append(pltpu.make_async_copy(src, buf.at[n], load_sem.at[base + n]))
-    loads.append(
-        pltpu.make_async_copy(short_ref, w_ref.at[chunks - 1], load_sem.at[len(lefts) + len(rights)])
-    )
-    due = [0] * len(loads)
-    for n in range(len(lefts)):
-        due[n] = left_at.index(n)
-    for n in range(len(rights)):
-        due[len(lefts) + n] = right_at.index(n)
-    due[-1] = chunks - 1
+            loads.append(pltpu.make_async_copy(src, buf.at[n], load_sem.at[len(loads)]))
+            first_use = at.index(n)
+            due.append(min(first_use, rest.FIRST) if at is right_at and n in taps[:3] else first_use)
+    for name, src, dst in zip(REST, rest_refs, kept):
+        loads.append(pltpu.make_async_copy(src, dst, load_sem.at[len(loads)]))
+        due.append(rest.due(name))
     for n in sorted(range(len(loads)), key=lambda n: (due[n], n)):
         loads[n].start()
 
@@ -535,7 +712,6 @@
     greet(F)
     pl.semaphore_wait(barrier, len(pairs) + F - 1)
     move = Move(False, F, piece_ref, slot_ref, sems)
-    move.start()
 
     cut = [TILE]
     for k in range(4):
@@ -629,6 +805,12 @@
             ones = jnp.ones((16, T), BF16)
             t_ref[pl.ds(pick(t, right_at), 1)] = dot(ones, right)[:1]
 
+        @pl.when(t == rest.weights_at)
+        def _():
+            move.start()
+
+        rest.step(t, piece_ref)
+
         @pl.when(t == chunks - 1)
         def _():
             w_ref[chunks - 1, pl.ds(used, t_ref.shape[0])] = t_ref[...].astype(BF16)
@@ -663,21 +845,24 @@
 
     lax.fori_loop(0, chunks, drain, 0)
     move.wait()
+    rest.drain()
     for c in range(chunks):
         out_copy(c).wait()
 
 
-def sum_everywhere(products, short, used, pieces, F, sizes, cid):
+def sum_everywhere(products, rest, taps, used, S, F, sizes, cid):
     arrays, lefts, rights = [], [], []
     places, left_at, right_at, shapes = [], [], [], []
 
     def slots_of(pieces, slots):
         found = []
         for array, width in pieces:
-            which = next((n for n, a in enumerate(arrays) if a is array), None)
-            if which is None:
-                which = len(arrays)
-                arrays.append(array)
+            which = None
+            if array is not None:
+                which = next((n for n, a in enumerate(arrays) if a is array), None)
+                if which is None:
+                    which = len(arrays)
+                    arrays.append(array)
             for col in range(0, width, TILE):
                 if (which, col) not in slots:
                     slots.append((which, col))
@@ -693,8 +878,10 @@
                 left_at.append(u)
                 right_at.append(v)
     places.append((len(products), 0, 0))
-    shapes.append(short.shape)
+    shapes.append((TILE, TILE))
     T = min(a.shape[0] for a in arrays)
+    R = rest["stem_linear"].shape[0]
+    mels = rest["columns"].shape[1] // 4
     chunks = len(places)
     cut = [TILE]
     for n in sizes:
@@ -703,14 +890,26 @@
         cut[4] = cut[3]
     most = max(sizes) - 1
     spec = pl.BlockSpec(memory_space=pl.ANY)
-    sums = len(rights) + -len(rights) % 16
-    plan = (places, left_at, right_at, lefts, rights, len(arrays) + 2, len(shapes) + 1)
+    sums = len(rights) + 5
+    sums += -sums % 16
+    slots = jax.ShapeDtypeStruct((S, T // S, 2 * mels), F32)
+    taps = tuple(right_at[n] for n in taps) + (len(rights),)
+    plan = (
+        places,
+        left_at,
+        right_at,
+        lefts,
+        rights,
+        len(arrays) + len(REST),
+        len(shapes) + 1,
+        taps,
+        T,
+    )
     return pl.pallas_call(
         functools.partial(sum_kernel, sizes, F, used, plan),
-        in_specs=[spec] * (len(arrays) + 2),
+        in_specs=[spec] * (len(arrays) + len(REST)),
         out_specs=[spec] * (len(shapes) + 1),
-        out_shape=[jax.ShapeDtypeStruct(v, BF16) for v in shapes]
-        + [jax.ShapeDtypeStruct(pieces.shape, pieces.dtype)],
+        out_shape=[jax.ShapeDtypeStruct(v, BF16) for v in shapes] + [slots],
         scratch_shapes=[
             pltpu.VMEM((len(lefts), T, TILE), BF16),
             pltpu.VMEM((len(rights), T, TILE), BF16),
@@ -718,17 +917,30 @@
         ]
         + [pltpu.VMEM((chunks, TILE, TILE), BF16)] * 2
         + [pltpu.VMEM((chunks, sizes[k] - 1, cut[k + 1], TILE), BF16) for k in range(4)]
+        + [pltpu.VMEM(rest[name].shape, rest[name].dtype) for name in REST]
+        + [
+            pltpu.VMEM((R + 16, TILE), BF16),
+            pltpu.VMEM((2, 16, TILE), BF16),
+            pltpu.VMEM((2, 16, TILE), BF16),
+            pltpu.VMEM((R, 2 * TILE), BF16),
+            pltpu.VMEM((R, 2 * mels), F32),
+            pltpu.VMEM((R + 8, 2 * mels), F32),
+            pltpu.VMEM((R, 2 * mels), F32),
+            pltpu.VMEM(slots.shape, F32),
+        ]
         + [
             pltpu.SemaphoreType.DMA((chunks, 8, most)),
             pltpu.SemaphoreType.DMA((chunks, 8, most)),
-            pltpu.SemaphoreType.DMA((len(lefts) + len(rights) + 1,)),
+            pltpu.SemaphoreType.DMA((len(lefts) + len(rights) + len(REST),)),
             pltpu.SemaphoreType.DMA((chunks,)),
+            pltpu.SemaphoreType.DMA((2,)),
+            pltpu.SemaphoreType.DMA((2,)),
         ]
-        + move_sems(pieces.shape[0]),
+        + move_sems(S),
         compiler_params=pltpu.CompilerParams(
-            collective_id=cid, has_side_effects=True, vmem_limit_bytes=60 << 20
+            collective_id=cid, has_side_effects=True, vmem_limit_bytes=67043328
         ),
-    )(*arrays, short, pieces)
+    )(*arrays, *[rest[name] for name in REST])
 
 
 def on_device(
@@ -860,90 +1072,78 @@
         block,
         F,
     )
-    query_grad, key_grad, value_grad = query_wide[:T], key_grad[:T], value_grad[:T]
-    normed_grad = (
-        dot_t(query_grad, query_weight)
-        + dot_t(key_grad, key_weight)
-        + dot_t(value_grad, value_weight)
-    )
-    inner, first_gain_grad, first_shift_grad = norm_pull(xhat1, r1, first_gain, normed_grad)
-    stream_grad = mixed_grad + inner
-    conv_grad = (gelu_slope(conv_linear) * stream_grad).astype(BF16)
-    conv_ext = with_halo(conv_grad)
-    conv_after = jnp.roll(conv_ext, -1, axis=0)
-    pair_grad = dot_t(conv_ext, reduce_matrix[D:])
-    third_grad = dot_t(conv_after, reduce_matrix[:D])
-    active_grad = pair_grad + jnp.concatenate([jnp.zeros_like(third_grad), third_grad], axis=1)
-    stem_grad = jnp.where(valid, gelu_slope(stem_linear) * active_grad, 0.0).astype(BF16)
-    own = stem_grad[:T]
-    totals = column_total(own)
-    stem_bias_grad = totals[:D] + totals[D:]
-    pair_matrix_grad = outer(columns[:T], own)
-    stem_matrix_grad = pair_matrix_grad[: 3 * mels, :D] + pair_matrix_grad[mels:, D:]
-    mel_columns = dot_t(stem_grad, stem_pair)
-    mel_pair = (
-        mel_columns[:, mels : 3 * mels]
-        + jnp.concatenate(
-            [
-                jnp.roll(mel_columns[:, 3 * mels :], 1, axis=0),
-                jnp.roll(mel_columns[:, :mels], -1, axis=0),
-            ],
-            axis=1,
-        )
-    )[:T]
+    key_grad, value_grad = key_grad[:T], value_grad[:T]
     sizes = (2, F // 2, F // 2, lax.axis_size("dp") // (F // 2))
-    small = [stem_bias_grad, first_gain_grad, first_shift_grad, second_gain_grad, second_shift_grad]
-    at = 3 * mels
-    used = at + len(small) + -(at + len(small)) % 16
-    short = jnp.pad(stem_matrix_grad, ((0, TILE - at), (0, 0)))
-    place = lax.broadcasted_iota(jnp.int32, (TILE, 1), 0)
-    for n, v in enumerate(small):
-        short = jnp.where(place == at + n, v[None, :], short)
+    used = 3 * mels + -3 * mels % 16
+    none = jnp.zeros((mels, 2 * D), BF16)
+    taps = [
+        stem_pair[mels : 3 * mels],
+        jnp.concatenate([stem_pair[3 * mels :], none], axis=0),
+        jnp.concatenate([none, stem_pair[:mels]], axis=0),
+    ]
+    rest = {
+        "query": query_weight,
+        "key": key_weight,
+        "value": value_weight,
+        "xhat": xhat1,
+        "r": jnp.broadcast_to(r1, (T, 128)),
+        "gain": jnp.broadcast_to(first_gain, (8, D)),
+        "mixed": mixed_grad,
+        "conv_linear": conv_linear,
+        "reduce": reduce_matrix,
+        "stem_linear": stem_linear,
+        "stem_taps": jnp.stack(taps),
+        "columns": columns,
+        "second": jnp.where(
+            lax.broadcasted_iota(jnp.int32, (8, 1), 0) == 0, second_gain_grad, second_shift_grad
+        ),
+    }
     FF = hidden_weight.shape[1]
+    wide = FF // D
     one = [(first_normed, D)]
     *terms, mel_slots = sum_everywhere(
         [
             ([(hidden_active, FF)], [(cot, D)]),
             ([(second_normed, D)], [(hidden_grad, FF)]),
             ([(attended, D)], [(branch_grad, D)]),
-            ([(odd_active_before, D), (stem_active, 2 * D)], [(conv_grad, D)]),
             (one, [(query_wide, D)]),
             (one, [(key_grad, D)]),
             (one, [(value_grad, D)]),
+            ([(odd_active_before, D), (stem_active, 2 * D)], [(None, D)]),
         ],
-        short.astype(BF16),
+        rest,
+        (2 * wide + 1, 2 * wide + 2, 2 * wide + 3, 2 * wide + 4),
         used,
-        mel_pair.reshape(S, piece, 2 * mels),
+        S,
         F,
         sizes,
         0,
     )
     mel_gradient = mel_slots.reshape(S, piece_frames, mels)
-    return_w, hidden_w, output_w, reduce_w, query_w, key_w, value_w, short = [
+    return_w, hidden_w, output_w, query_w, key_w, value_w, reduce_w, short = [
         v.astype(F32) for v in terms
     ]
     stem_w = short[: 3 * mels]
-    small = [short[at + n] for n in range(len(small))]
     sums = short[used:]
-    wide = FF // D
+    small = wide + 6
     return (
         layer_output,
         mel_gradient,
         stem_w.reshape(3, mels, D),
-        small[0],
+        sums[small],
         reduce_w.reshape(3, D, D),
+        sums[wide + 5],
+        sums[small + 1],
+        sums[small + 2],
+        query_w,
         sums[wide + 2],
-        small[1],
-        small[2],
-        query_w,
-        sums[wide + 3],
         key_w,
         value_w,
-        sums[wide + 5],
+        sums[wide + 4],
         output_w,
         sums[wide + 1],
-        small[3],
-        small[4],
+        sums[small + 3],
+        sums[small + 4],
         hidden_w,
         sums[1 : wide + 1].reshape(FF),
         return_w,

time: 258 us -> 243 us (0.942)
  matrix products: 46.1 us -> 33.8 us
  Pallas kernels: 147 us -> 154 us
  starting transfers between devices: 12.5 us -> 8.96 us
  local copies, waits for them, and re-layouts: 21.3 us -> 18.2 us
    dot_general x9 -> x3, matrix products: 19.7 us -> 10 us  [dot_t(): lax.dot_general(left, right, (((1,), (1,)), ((), ())), preferred_element_...]
    pallas_call x1, Pallas kernels: 90.9 us -> 97.7 us  [sum_everywhere(): pl.pallas_call(functools.partial(sum_kernel, sizes, F, used, plan), in_sp...]
    convert_element_type x2 -> x0, other arithmetic: 3.42 us -> none  [the longest x1 1.99 us: on_device(): conv_grad = (gelu_slope(conv_linear) * stream_grad).astype(BF16)]
    unnamed x103 -> x79, local copies, waits for them, and re-layouts: 11.1 us -> 8.09 us
  transfers between devices with their start and end apart: 6 -> 4, of which waited for: 2 -> 2; matrix products, arithmetic and copies ran while one was open for 2% -> 1% of each run, Pallas kernels for 0% -> 0%
where the time goes in v1:
time: 243 us; the launch traced here: 242 us
  Pallas kernels  154 us (63%)
  matrix products  33.8 us (14%)
  other arithmetic  21.4 us (9%)
  local copies, waits for them, and re-layouts  18.2 us (7%)
  starting transfers between devices  8.96 us (4%)
  waiting for transfers between devices  3.49 us (1%)
    pallas_call x1, Pallas kernels, sum_everywhere(): pl.pallas_call(functools.partial(sum_kernel, sizes, F, used, plan), in_sp...  97.7 us
    pallas_call x1, Pallas kernels, attn_bwd(): pl.pallas_call(functools.partial(bwd_kernel, scale, hd, F, G, pairs), gri...  29 us
    pallas_call x1, Pallas kernels, attn_fwd(): pl.pallas_call(functools.partial(fwd_kernel, scale, hd, F, G, T, pairs),...  27.3 us
    dot_general x8, matrix products, dot(): return jnp.dot(left, right, preferred_element_type=F32)  23.8 us
    convert_element_type x7, other arithmetic, on_device(): v.astype(F32)  10.9 us
    dot_general x3, matrix products, dot_t(): lax.dot_general(left, right, (((1,), (1,)), ((), ())), preferred_element_...  10 us
    unnamed x79, local copies, waits for them, and re-layouts  8.09 us
    ppermute x2, starting transfers between devices, gather_window(): got = lax.ppermute(part, 'frame', perm)  4.9 us
  transfers between devices with their start and end apart: 4, of which 2 were waited for; matrix products, arithmetic and copies ran while one was open for 1% of the time, Pallas kernels for 0%

profile of v1, /device:TPU:0, one launch (start us, length us, event | category | flops | bytes accessed | tf_op | source)
XLA Modules:
  0.0 241.8 jit_solution(18335711666374208018)
XLA Ops:
  0.7 1.2 copy.44
  2.2 0.7 collective-permute-start
  2.9 4.2 %collective-permute-start.1 = (bf16[376,160]{1,0:T(8,128)(2,1)S(1)}, bf16[376,160]{1,0:T(8,128)(2,1)S(1)}, u32[]{:S(2)}, u32[]{:S(2)}) collective-permute-start(bf16[376,160]{1,0:T(8,128)(2,1)S(1)} %get-tuple-element.123), channel_id=1, source_target_pairs={{0,2},{1,0},{2,3},{3,1},{4,6},{5,4},{6,7},{7,5},{8,10},{9,8},{10,1... | collective-permute-start | bytes 360968 | tf_op jit(solution)/shard_map/ppermute | solution.py:990
  7.8 1.1 pad_maximum_fusion.refs_22_
  9.2 2.5 %collective-permute-done.1 = bf16[376,160]{1,0:T(8,128)(2,1)S(1)} collective-permute-done((bf16[376,160]{1,0:T(8,128)(2,1)S(1)}, bf16[376,160]{1,0:T(8,128)(2,1)S(1)}, u32[]{:S(2)}, u32[]{:S(2)}) %collective-permute-start.1) | collective-permute-done | bytes 120352 | tf_op jit(solution)/shard_map/ppermute | solution.py:990
  11.7 2.8 %collective-permute-start.2 = (bf16[1,160]{1,0:T(2,128)(2,1)S(1)}, bf16[1,160]{1,0:T(2,128)(2,1)S(1)}, u32[]{:S(2)}, u32[]{:S(2)}) collective-permute-start(bf16[1,160]{1,0:T(2,128)(2,1)S(1)} %get-tuple-element.122), channel_id=1, source_target_pairs={{0,1},{2,3},{4,5},{6,7},{8,9},{10,11},{12,13},{14,15},{16,17},{18,... | collective-permute-start | bytes 968 | tf_op jit(solution)/shard_map/ppermute | solution.py:999
  14.5 1.3 collective-permute-start.3
  16.6 1.0 collective-permute-done.3
  17.6 5.1 %fusion.5 = (bf16[768,1024]{1,0:T(8,128)(2,1)S(1)}, f32[768,1024]{1,0:T(8,128)}) fusion(pred[768]{0:T(1024)(128)(4,1)S(1)} %fusion.25, f32[1024]{0:T(1024)S(1)} %pad_maximum_fusion.7, bf16[240,512]{1,0:T(8,128)(2,1)S(1)} %bitcast.64, bf16[1,160]{1,0:T(2,128)(2,1)S(1)} %collective-permute-done.2, bf16[14,160]{1,0:T(8,128)(2,1)S(1)} %broadcast_in_dim.34, ...), kind=kOutput, calls=%fused_computation.15 | convolution fusion | flops 531988480 | bytes 5215296 | tf_op jit(solution)/shard_map/dot_general | solution.py:49
  22.9 0.9 copy-done
  24.0 0.6 copy-done.10
  24.7 3.8 %fusion.32 = (f32[752]{0:T(1024)S(1)}, f32[752,512]{1,0:T(8,128)S(1)}, f32[752,512]{1,0:T(8,128)}) fusion(f32[752,256]{1,0:T(8,128)S(1)} %bitcast.60, f32[752,256]{1,0:T(8,128)S(1)} %bitcast.59, f32[512]{0:T(512)S(1)} %copy-done.33, bf16[1536,512]{1,0:T(8,128)(2,1)S(1)} %bitcast.57, bf16[752,1024]{1,0:T(8,128)(2,1)S(1)} %slice.141, ...), kind=kOutput, calls=%fused_computation.97 | convolution fusion | flops 1197423872 | bytes 8508352 | tf_op jit(solution)/shard_map/dot_general | solution.py:49
  29.2 1.5 add_convert_fusion.3
  30.7 0.6 add_convert_fusion.2
  31.3 0.9 pad.11.q_ref
  32.2 1.4 convolution_convert_fusion.1.k_own
  33.6 1.4 add_convert_fusion.1.v_own
  35.1 27.3 %shard_map.373 = (bf16[8,1504,768]{2,1,0:T(8,128)(2,1)}, f32[768,512]{1,0:T(8,128)}, bf16[1504,512]{1,0:T(8,128)(2,1)}, bf16[1504,512]{1,0:T(8,128)(2,1)}, bf16[2,376,512]{2,1,0:T(8,128)(2,1)}) custom-call(bf16[768,512]{1,0:T(8,128)(2,1)} %pad.11.q_ref, bf16[752,512]{1,0:T(8,128)(2,1)} %convolution_convert_fusion.1.k_own, ...), custom_call_target="tpu_custom_call" | custom-call | tf_op jit(solution)/shard_map/pallas_call | solution.py:291
  62.4 2.5 %slice.161.refs_4_ = bf16[752,512]{1,0:T(8,128)(2,1)} slice(f32[768,512]{1,0:T(8,128)} %get-tuple-element.40.o_ref), slice={[0:752], [0:512]} | slice | bytes 1540096 | tf_op jit(solution)/shard_map/slice | solution.py:1043
  64.9 2.0 fusion.37
  67.3 0.7 copy-done.14
  68.5 1.5 copy-done.30
  70.0 6.8 %multiply_convert_fusion = (bf16[752,2048]{1,0:T(8,128)(2,1)S(1)}, f32[752,2048]{1,0:T(8,128)S(1)}) fusion(f32[2048]{0:T(1024)S(1)} %copy-done.32, bf16[752,512]{1,0:T(8,128)(2,1)S(1)} %add_convert_fusion.refs_2_, bf16[512,2048]{1,0:T(8,128)(2,1)S(1)} %copy-done.30), kind=kOutput, calls=%fused_computation.3 | convolution fusion | flops 1614020608 | bytes 12115968 | tf_op jit(solution)/shard_map/dot_general | solution.py:49
  76.8 7.2 %multiply_convert_fusion.1.refs_3_ = bf16[752,2048]{1,0:T(8,128)(2,1)S(1)} fusion(f32[752,2048]{1,0:T(8,128)S(1)} %get-tuple-element.138, bf16[752,512]{1,0:T(8,128)(2,1)S(1)} %bitcast.54, bf16[2048,512]{1,0:T(8,128)(2,1)S(1)} %copy-done.31, f32[2048]{0:T(1024)S(1)} %copy-done.32), kind=kOutput, calls=%fused_computation.4 | convolution fusion | flops 1618640896 | bytes 12115968 | tf_op jit(solution)/shard_map/dot_general | solution.py:53
  84.0 2.2 multiply_reduce_fusion
  86.3 1.8 fusion.31
  88.1 0.6 convolution_convert_fusion
  88.7 0.9 pad.12.do_ref
  89.7 2.6 %select_convert_fusion = bf16[752,512]{1,0:T(8,128)(2,1)} fusion(f32[752,512]{1,0:T(8,128)S(1)} %get-tuple-element.135, bf16[752,2048]{1,0:T(8,128)(2,1)S(1)} %get-tuple-element.137.refs_0_, bf16[2048,512]{1,0:T(8,128)(2,1)S(1)} %copy-done.31, f32[512]{0:T(512)S(1)} %copy-done.36, pred[]{:T(512)S(6)} %lt.57), kind=kOutput, calls=%fused_computation.29 | convolution fusion | flops 1578598400 | bytes 7489537 | tf_op jit(solution)/shard_map/dot_general | solution.py:49
  92.3 0.7 broadcast_select_fusion.1.refs_24_
  93.0 29.0 %shard_map.374 = (bf16[768,512]{1,0:T(8,128)(2,1)}, bf16[752,512]{1,0:T(8,128)(2,1)}, bf16[752,512]{1,0:T(8,128)(2,1)}, bf16[2,376,512]{2,1,0:T(8,128)(2,1)}) custom-call(bf16[768,512]{1,0:T(8,128)(2,1)} %pad.11.q_ref, bf16[768,512]{1,0:T(8,128)(2,1)} %pad.12.do_ref, f32[768,512]{1,0:T(8,128)} %get-tuple-element.40.o_ref, ...), custom_call_target="tpu_custom_call" | custom-call | tf_op jit(solution)/shard_map/pallas_call | solution.py:443
  122.0 1.5 fusion.21.refs_23_
  123.5 0.9 broadcast_in_dim.37.refs_16_
  124.4 0.6 broadcast_in_dim.38.refs_17_
  125.0 97.7 %shard_map.375 = (bf16[2048,512]{1,0:T(8,128)(2,1)}, bf16[512,2048]{1,0:T(8,128)(2,1)}, bf16[512,512]{1,0:T(8,128)(2,1)}, bf16[512,512]{1,0:T(8,128)(2,1)}, bf16...) custom-call(bf16[752,2048]{1,0:T(8,128)(2,1)} %copy-done.2, ...), custom_call_target="tpu_custom_call" | custom-call | tf_op jit(solution)/shard_map/pallas_call | solution.py:908
  222.7 1.3 convert_element_type.96
  224.0 1.8 slice.146
  225.8 1.6 fusion.35
  227.4 2.5 %convert_element_type.101 = f32[512,2048]{1,0:T(8,128)} convert(bf16[512,2048]{1,0:T(8,128)(2,1)S(1)} %copy-done.9) | non-fusion elementwise | flops 1048576 | bytes 6291456 | tf_op jit(solution)/shard_map/convert_element_type | solution.py:1124
  230.0 2.6 %convert_element_type.102 = f32[2048,512]{1,0:T(8,128)} convert(bf16[2048,512]{1,0:T(8,128)(2,1)S(1)} %copy-done.8) | non-fusion elementwise | flops 1048576 | bytes 6291456 | tf_op jit(solution)/shard_map/convert_element_type | solution.py:1124
  232.6 2.1 convert.5
  234.9 1.0 copy.45
  235.9 0.6 copy.46
  236.5 1.1 convert_element_type.100
  237.7 1.1 convert_element_type.97
  238.8 1.1 convert_element_type.98
  239.9 1.1 convert_element_type.99
  241.0 0.9 copy.51
  (109 shorter events, 3.3 us)
Async XLA Ops:
  0.7 6.5 %copy-start.23 = (bf16[3,80,512]{2,1,0:T(8,128)(2,1)S(1)}, bf16[3,80,512]{2,1,0:T(8,128)(2,1)}, u32[]{:S(2)}) copy-start(bf16[3,80,512]{2,1,0:T(8,128)(2,1)} %param.24) | copy-start | bytes 737284
  2.1 5.1 %copy-start.29 = (f32[512]{0:T(512)S(1)}, f32[512]{0:T(512)}, u32[]{:S(2)}) copy-start(f32[512]{0:T(512)} %param.25) | copy-start | bytes 6148
  2.2 6.9 %collective-permute-start = (bf16[376,160]{1,0:T(8,128)(2,1)S(1)}, bf16[376,160]{1,0:T(8,128)(2,1)S(1)}, u32[]{:S(2)}, u32[]{:S(2)}) collective-permute-start(bf16[376,160]{1,0:T(8,128)(2,1)S(1)} %get-tuple-element.124), channel_id=1, source_target_pairs={{0,0},{1,2},{2,1},{3,3},{4,4},{5,6},{6,5},{7,7},{8,8},{9,10},{10,9... | collective-permute-start | bytes 360968 | tf_op jit(solution)/shard_map/ppermute | solution.py:990
  2.9 8.8 %collective-permute-start.1 = (bf16[376,160]{1,0:T(8,128)(2,1)S(1)}, bf16[376,160]{1,0:T(8,128)(2,1)S(1)}, u32[]{:S(2)}, u32[]{:S(2)}) collective-permute-start(bf16[376,160]{1,0:T(8,128)(2,1)S(1)} %get-tuple-element.123), channel_id=1, source_target_pairs={{0,2},{1,0},{2,3},{3,1},{4,6},{5,4},{6,7},{7,5},{8,10},{9,8},{10,1... | collective-permute-start | bytes 360968 | tf_op jit(solution)/shard_map/ppermute | solution.py:990
  11.7 4.7 %collective-permute-start.2 = (bf16[1,160]{1,0:T(2,128)(2,1)S(1)}, bf16[1,160]{1,0:T(2,128)(2,1)S(1)}, u32[]{:S(2)}, u32[]{:S(2)}) collective-permute-start(bf16[1,160]{1,0:T(2,128)(2,1)S(1)} %get-tuple-element.122), channel_id=1, source_target_pairs={{0,1},{2,3},{4,5},{6,7},{8,9},{10,11},{12,13},{14,15},{16,17},{18,... | collective-permute-start | bytes 968 | tf_op jit(solution)/shard_map/ppermute | solution.py:999
  14.5 3.1 %collective-permute-start.3 = (bf16[1,160]{1,0:T(2,128)(2,1)S(1)}, bf16[1,160]{1,0:T(2,128)(2,1)S(1)}, u32[]{:S(2)}, u32[]{:S(2)}) collective-permute-start(bf16[1,160]{1,0:T(2,128)(2,1)S(1)} %get-tuple-element.121), channel_id=1, source_target_pairs={{1,0},{3,2},{5,4},{7,6},{9,8},{11,10},{13,12},{15,14},{17,16},{19,... | collective-permute-start | bytes 968 | tf_op jit(solution)/shard_map/ppermute | solution.py:1000
  22.7 1.2 copy-start
  22.7 1.9 copy-start.10
  23.8 0.8 copy-start.33
  24.0 4.5 %copy-start.6 = (bf16[752,512]{1,0:T(8,128)(2,1)}, bf16[752,512]{1,0:T(8,128)(2,1)S(1)}, u32[]{:S(2)}) copy-start(bf16[752,512]{1,0:T(8,128)(2,1)S(1)} %pad_maximum_fusion.1.refs_10_) | copy-start | bytes 2310148
  28.5 0.7 copy-start.25
  28.5 0.7 copy-start.26
  29.2 1.5 copy-start.15
  29.2 1.5 copy-start.34
  30.7 3.0 %copy-start.4 = (bf16[752,512]{1,0:T(8,128)(2,1)}, bf16[752,512]{1,0:T(8,128)(2,1)S(1)}, u32[]{:S(2)}) copy-start(bf16[752,512]{1,0:T(8,128)(2,1)S(1)} %get-tuple-element.105.refs_6_) | copy-start | bytes 2310148
  30.7 1.5 copy-start.16
  31.2 2.4 copy-start.17
  31.3 2.4 copy-start.35
  62.4 2.5 %copy-start.22 = (bf16[512,512]{1,0:T(8,128)(2,1)S(1)}, bf16[512,512]{1,0:T(8,128)(2,1)}, u32[]{:S(2)}) copy-start(bf16[512,512]{1,0:T(8,128)(2,1)} %param.35) | copy-start | bytes 1572868
  62.4 2.5 %copy-start.27 = (f32[512]{0:T(512)S(1)}, f32[512]{0:T(512)}, u32[]{:S(2)}) copy-start(f32[512]{0:T(512)} %param.36) | copy-start | bytes 6148
  66.9 1.1 copy-start.14
  66.9 1.2 copy-start.24
  66.9 1.2 copy-start.28
  68.1 18.2 %copy-start.1 = (bf16[2,376,512]{2,1,0:T(8,128)(2,1)}, bf16[2,376,512]{2,1,0:T(8,128)(2,1)S(1)}, u32[]{:S(2)}) copy-start(bf16[2,376,512]{2,1,0:T(8,128)(2,1)S(1)} %broadcast_select_fusion) | copy-start | bytes 2310148
  68.1 1.9 copy-start.30
  68.1 1.9 copy-start.32
  70.0 6.8 %copy-start.5 = (bf16[752,512]{1,0:T(8,128)(2,1)}, bf16[752,512]{1,0:T(8,128)(2,1)S(1)}, u32[]{:S(2)}) copy-start(bf16[752,512]{1,0:T(8,128)(2,1)S(1)} %add_convert_fusion.refs_2_) | copy-start | bytes 2310148
  70.0 6.8 %copy-start.31 = (bf16[2048,512]{1,0:T(8,128)(2,1)S(1)}, bf16[2048,512]{1,0:T(8,128)(2,1)}, u32[]{:S(2)}) copy-start(bf16[2048,512]{1,0:T(8,128)(2,1)} %param.41) | copy-start | bytes 6291460
  76.8 12.9 %copy-start.2 = (bf16[752,2048]{1,0:T(8,128)(2,1)}, bf16[752,2048]{1,0:T(8,128)(2,1)S(1)}, u32[]{:S(2)}) copy-start(bf16[752,2048]{1,0:T(8,128)(2,1)S(1)} %get-tuple-element.137.refs_0_) | copy-start | bytes 9240580
  84.0 2.3 copy-start.3
  88.1 1.5 copy-start.7
  88.1 1.5 copy-start.36
  222.7 4.7 %copy-start.9 = (bf16[512,2048]{1,0:T(8,128)(2,1)S(1)}, bf16[512,2048]{1,0:T(8,128)(2,1)}, u32[]{:S(2)}) copy-start(bf16[512,2048]{1,0:T(8,128)(2,1)} %get-tuple-element.55) | copy-start | bytes 6291460
  227.4 2.6 %copy-start.8 = (bf16[2048,512]{1,0:T(8,128)(2,1)S(1)}, bf16[2048,512]{1,0:T(8,128)(2,1)}, u32[]{:S(2)}) copy-start(bf16[2048,512]{1,0:T(8,128)(2,1)} %get-tuple-element.56) | copy-start | bytes 6291460
  230.0 2.6 %copy-start.11 = (bf16[1536,512]{1,0:T(8,128)(2,1)S(1)}, bf16[1536,512]{1,0:T(8,128)(2,1)}, u32[]{:S(2)}) copy-start(bf16[1536,512]{1,0:T(8,128)(2,1)} %get-tuple-element.50) | copy-start | bytes 4718596
  232.6 2.1 copy-start.13
  234.7 1.8 copy-start.21
  234.9 2.8 %copy-start.20 = (bf16[512,512]{1,0:T(8,128)(2,1)S(1)}, bf16[512,512]{1,0:T(8,128)(2,1)}, u32[]{:S(2)}) copy-start(bf16[512,512]{1,0:T(8,128)(2,1)} %get-tuple-element.51) | copy-start | bytes 1572868
  236.5 2.2 copy-start.19
  237.7 2.2 copy-start.18
  238.8 2.2 copy-start.12

commit v2 on v1

--- a/solution.py
+++ b/solution.py
@@ -175,6 +175,88 @@
     return pl.ds(pl.multiple_of(pair * 128, 128), 128)
 
 
+def mel_kernel(F, m_ref, e_ref, d_ref, h_ref, edge_send, edge_recv, edge_own, *sems):
+    S = m_ref.shape[0]
+    G = F // S
+    dp, fr = lax.axis_index("dp"), lax.axis_index("frame")
+    r = lax.rem(fr, G)
+    meet(F)
+    move = Move(True, F, m_ref, d_ref, sems)
+    ends = []
+    for a in range(S):
+        last = (lax.rem(fr, S) == S - 1) & (fr + 1 < F)
+        ends.append((a, 0, last, a * G + (fr + 1) // S))
+        first = (lax.rem(fr, S) == 0) & (fr > 0)
+        ends.append((a, 1, first, a * G + fr // S - 1))
+
+    def far(a, k, to):
+        return pltpu.make_async_remote_copy(
+            src_ref=e_ref.at[a, k],
+            dst_ref=h_ref.at[k],
+            send_sem=edge_send.at[k, a],
+            recv_sem=edge_recv.at[k],
+            device_id=(dp, to),
+            device_id_type=MESH,
+        )
+
+    def near(a, k):
+        return pltpu.make_async_copy(e_ref.at[a, k], h_ref.at[k], edge_own.at[k])
+
+    for a, k, holds, to in ends:
+
+        @pl.when(holds & (to != fr))
+        def _():
+            far(a, k, to).start()
+
+        @pl.when(holds & (to == fr))
+        def _():
+            near(a, k).start()
+
+    move.start()
+    for a, k, holds, to in ends:
+
+        @pl.when(holds & (to != fr))
+        def _():
+            far(a, k, to).wait_send()
+
+        @pl.when(holds & (to == fr))
+        def _():
+            near(a, k).wait()
+
+    for k, wanted, sender in ((0, r > 0, r * S - 1), (1, r < G - 1, (r + 1) * S)):
+
+        @pl.when(wanted & (sender != fr))
+        def _():
+            landed = h_ref.at[k]
+            pltpu.make_async_copy(landed, landed, edge_recv.at[k]).wait()
+
+    move.wait()
+
+
+def gather_mel(pairs, F):
+    S, piece, width = pairs.shape
+    edges = jnp.stack([pairs[:, piece - 8 :], pairs[:, :8]], axis=1)
+    far = pl.BlockSpec(memory_space=pl.ANY)
+    return pl.pallas_call(
+        functools.partial(mel_kernel, F),
+        in_specs=[far, far],
+        out_specs=[far, far],
+        out_shape=[
+            jax.ShapeDtypeStruct(pairs.shape, pairs.dtype),
+            jax.ShapeDtypeStruct((2, 8, width), pairs.dtype),
+        ],
+        scratch_shapes=[
+            pltpu.SemaphoreType.DMA((2, S)),
+            pltpu.SemaphoreType.DMA((2,)),
+            pltpu.SemaphoreType.DMA((2,)),
+        ]
+        + move_sems(S),
+        compiler_params=pltpu.CompilerParams(
+            collective_id=3, has_side_effects=True, vmem_limit_bytes=1 << 20
+        ),
+    )(pairs, edges)
+
+
 def fwd_kernel(
     scale,
     hd,
@@ -188,6 +270,7 @@
     c_ref,
     p_ref,
     o_ref,
+    b_ref,
     k_all,
     v_all,
     d_ref,
@@ -267,7 +350,9 @@
         p = (e * (1.0 / l)).astype(BF16)
         p_ref[h] = p
         outs.append(jnp.dot(vt[h * hd : (h + 1) * hd], p, preferred_element_type=F32))
-    o_ref[...] = jnp.concatenate(outs, axis=0).T
+    out = jnp.concatenate(outs, axis=0).T
+    o_ref[...] = out
+    b_ref[...] = out.astype(BF16)
 
     @pl.when((pair == pairs - 1) & (i == pl.num_programs(1) - 1))
     def _():
@@ -295,6 +380,7 @@
         out_specs=[
             pl.BlockSpec((per, N, QB), lambda p, i: (p, 0, i)),
             pl.BlockSpec((QB, 128), lambda p, i: (i, p)),
+            pl.BlockSpec((QB, 128), lambda p, i: (i, p)),
             far,
             far,
             far,
@@ -302,6 +388,7 @@
         out_shape=[
             jax.ShapeDtypeStruct((heads, N, R), BF16),
             jax.ShapeDtypeStruct((R, D), F32),
+            jax.ShapeDtypeStruct((R, D), BF16),
             jax.ShapeDtypeStruct((N, D), BF16),
             jax.ShapeDtypeStruct((N, D), BF16),
             jax.ShapeDtypeStruct(slots.shape, slots.dtype),
@@ -480,7 +567,7 @@
 
 
 class Rest:
-    FIRST = 2
+    FIRST = 5
 
     def __init__(self, G, T, taps, m_ref, t_ref, w_ref, data, scratch, sems):
         self.m, self.t, self.w = m_ref, t_ref, w_ref
@@ -502,7 +589,7 @@
     def due(self, name):
         if name in ("reduce", "stem_linear", "stem_taps"):
             return self.stem_at
-        if name in ("columns", "second"):
+        if name in ("columns", "second_gain", "second_shift"):
             return self.weights_at
         return self.FIRST
 
@@ -515,9 +602,8 @@
             + dot_t(self.m[k, rows], data["key"][...])
             + dot_t(self.m[v, rows], data["value"][...])
         )
-        xhat = data["xhat"][rows]
-        r = data["r"][rows][:, :1]
-        dh = dy * data["gain"][...][:1]
+        xhat, r = norm_parts(data["stream"][rows])
+        dh = dy * data["gain"][...]
         inner = r * (
             dh
             - jnp.mean(dh, axis=-1, keepdims=True)
@@ -613,7 +699,8 @@
             wide[: 3 * mels, :D] + wide[mels:, D:]
         ).astype(BF16)
         self.t[base : base + 1] = sums[:, :D] + sums[:, D:]
-        self.t[base + 3 : base + 5] = self.data["second"][...][:2]
+        self.t[base + 3 : base + 4] = self.data["second_gain"][...]
+        self.t[base + 4 : base + 5] = self.data["second_shift"][...]
 
     def step(self, t, out):
         todo = [(self.FIRST + n, functools.partial(self.tokens, n)) for n in range(len(self.token_blocks))]
@@ -639,8 +726,7 @@
     "query",
     "key",
     "value",
-    "xhat",
-    "r",
+    "stream",
     "gain",
     "mixed",
     "conv_linear",
@@ -648,7 +734,8 @@
     "stem_linear",
     "stem_taps",
     "columns",
-    "second",
+    "second_gain",
+    "second_shift",
 )
 
 
@@ -943,6 +1030,67 @@
     )(*arrays, *[rest[name] for name in REST])
 
 
+def widen_kernel(parts, count, *refs):
+    ins, outs = refs[:count], refs[count : 2 * count + 1]
+    b_ref, f_ref, load_sem, out_sem = refs[2 * count + 1 :]
+    loads, stores = [], []
+    for n, (which, row, col, places) in enumerate(parts):
+        rows = pl.ds(row, TILE)
+        cols = pl.ds(col, TILE)
+        loads.append(
+            pltpu.make_async_copy(ins[which].at[rows, cols], b_ref.at[n], load_sem.at[n])
+        )
+        here = []
+        for out, at, first, size in places:
+            target = outs[out].at[pl.ds(at, size), cols]
+            source = f_ref.at[n, pl.ds(first, size)]
+            here.append(pltpu.make_async_copy(source, target, out_sem.at[n, len(here)]))
+        stores.append(here)
+    for load in loads:
+        load.start()
+    for n, load in enumerate(loads):
+        load.wait()
+
+        def body(i, _):
+            rows = pl.ds(pl.multiple_of(i * 64, 64), 64)
+            f_ref[n, rows] = b_ref[n, rows].astype(F32)
+            return 0
+
+        lax.fori_loop(0, TILE // 64, body, 0)
+        for store in stores[n]:
+            store.start()
+    for here in stores:
+        for store in here:
+            store.wait()
+
+
+def widen(arrays, used, sums):
+    parts = []
+    last = len(arrays) - 1
+    for n, a in enumerate(arrays):
+        for row in range(0, a.shape[0], TILE):
+            for col in range(0, a.shape[1], TILE):
+                places = [(n, row, 0, TILE)]
+                if n == last:
+                    places = [(n, 0, 0, used[0]), (n + 1, 0, used[1], sums)]
+                parts.append((n, row, col, places))
+    shapes = [a.shape for a in arrays[:-1]] + [(used[0], TILE), (sums, TILE)]
+    far = pl.BlockSpec(memory_space=pl.ANY)
+    return pl.pallas_call(
+        functools.partial(widen_kernel, parts, len(arrays)),
+        in_specs=[far] * len(arrays),
+        out_specs=[far] * len(shapes),
+        out_shape=[jax.ShapeDtypeStruct(v, F32) for v in shapes],
+        scratch_shapes=[
+            pltpu.VMEM((len(parts), TILE, TILE), BF16),
+            pltpu.VMEM((len(parts), TILE, TILE), F32),
+            pltpu.SemaphoreType.DMA((len(parts),)),
+            pltpu.SemaphoreType.DMA((len(parts), 2)),
+        ],
+        compiler_params=pltpu.CompilerParams(vmem_limit_bytes=67043328),
+    )(*arrays)
+
+
 def on_device(
     mel_frames,
     window_count,
@@ -981,28 +1129,11 @@
     r = f % G
     alive = s < window_count[0]
 
-    def gather_window(x):
-        parts = []
-        out = jnp.zeros((S * x.shape[1], x.shape[2]), x.dtype)
-        for t in range(S):
-            part = lax.dynamic_index_in_dim(x, (f + t) % S, 0, keepdims=False)
-            perm = [(p, ((p % S + t) % S) * G + p // S) for p in range(F)]
-            got = lax.ppermute(part, "frame", perm)
-            j = (s - t) % S
-            out = lax.dynamic_update_slice(out, got, (j * x.shape[1], 0))
-        return out
-
-    down = [(i, i + 1) for i in range(F) if (i + 1) % G != 0]
-    up = [(i + 1, i) for i in range(F) if (i + 1) % G != 0]
-
-    def with_halo(x):
-        before = lax.ppermute(x[T - 1 : T], "frame", down)
-        after = lax.ppermute(x[0:1], "frame", up)
-        gap = jnp.zeros((R - T - 2, x.shape[1]), x.dtype)
-        return jnp.concatenate([x, after, gap, before], axis=0)
-
-    mel = gather_window(mel_frames.reshape(S, piece, 2 * mels))
-    mel = with_halo(mel)
+    own, beside = gather_mel(mel_frames.reshape(S, piece, 2 * mels), F)
+    before = jnp.where(r > 0, beside[0, -1:], jnp.zeros((1, 2 * mels), BF16))
+    after = jnp.where(r < G - 1, beside[1, :1], jnp.zeros((1, 2 * mels), BF16))
+    gap = jnp.zeros((R - T - 2, 2 * mels), BF16)
+    mel = jnp.concatenate([own.reshape(T, 2 * mels), after, gap, before], axis=0)
     odd_before = jnp.roll(mel[:, mels:], 1, axis=0)
     even_after = jnp.roll(mel[:, :mels], -1, axis=0)
     columns = jnp.concatenate([odd_before, mel, even_after], axis=1)
@@ -1027,21 +1158,19 @@
     conv_linear = dot(conv_columns, reduce_matrix) + reduce_bias
     stream = gelu(conv_linear) + positions_of(r * T, T, D)
     xhat1, r1 = norm_parts(stream)
-    first_normed = (xhat1 * first_gain + first_shift).astype(BF16)
-    query = (dot(first_normed, query_weight) + query_bias).astype(BF16)
-    key = dot(first_normed, key_weight).astype(BF16)
-    value = (dot(first_normed, value_weight) + value_bias).astype(BF16)
+    first_normed = jnp.pad((xhat1 * first_gain + first_shift).astype(BF16), ((0, R - T), (0, 0)))
+    query_ext = (dot(first_normed, query_weight) + query_bias).astype(BF16)
+    key = dot(first_normed[:T], key_weight).astype(BF16)
+    value = (dot(first_normed[:T], value_weight) + value_bias).astype(BF16)
     key = jnp.pad(key, ((0, -T % 16), (0, 0)))
     value = jnp.pad(value, ((0, -T % 16), (0, 0)))
-    query_ext = jnp.pad(query, ((0, R - T), (0, 0)))
     block = 256 if R % 256 == 0 else 128
-    probs, attended_wide, key_all, value_all, cot = attn_fwd(
+    probs, attended_wide, attended, key_all, value_all, cot = attn_fwd(
         query_ext, key, value, cotangent, scale, HEADS, block, F, T
     )
     cot = cot.reshape(T, D)
     cot = jnp.where(alive, cot, jnp.zeros_like(cot))
-    attended = attended_wide[:T].astype(BF16)
-    mixed = stream + dot(attended, output_weight) + output_bias
+    mixed = stream + dot(attended[:T], output_weight) + output_bias
     xhat2, r2 = norm_parts(mixed)
     second_normed = (xhat2 * second_gain + second_shift).astype(BF16)
     hidden_linear = dot(second_normed, hidden_weight) + hidden_bias
@@ -1056,9 +1185,9 @@
         xhat2, r2, second_gain, dot_t(hidden_grad, hidden_weight)
     )
     mixed_grad = cot.astype(F32) + inner
-    branch_grad = mixed_grad.astype(BF16)
-
-    attended_grad = jnp.pad(dot_t(branch_grad, output_weight).astype(BF16), ((0, R - T), (0, 0)))
+    branch_grad = jnp.pad(mixed_grad.astype(BF16), ((0, R - T), (0, 0)))
+
+    attended_grad = dot_t(branch_grad, output_weight).astype(BF16)
     query_wide, key_grad, value_grad, layer_output = attn_bwd(
         query_ext,
         attended_grad,
@@ -1085,18 +1214,16 @@
         "query": query_weight,
         "key": key_weight,
         "value": value_weight,
-        "xhat": xhat1,
-        "r": jnp.broadcast_to(r1, (T, 128)),
-        "gain": jnp.broadcast_to(first_gain, (8, D)),
+        "stream": stream,
+        "gain": first_gain.reshape(1, D),
         "mixed": mixed_grad,
         "conv_linear": conv_linear,
         "reduce": reduce_matrix,
         "stem_linear": stem_linear,
         "stem_taps": jnp.stack(taps),
         "columns": columns,
-        "second": jnp.where(
-            lax.broadcasted_iota(jnp.int32, (8, 1), 0) == 0, second_gain_grad, second_shift_grad
-        ),
+        "second_gain": second_gain_grad.reshape(1, D),
+        "second_shift": second_shift_grad.reshape(1, D),
     }
     FF = hidden_weight.shape[1]
     wide = FF // D
@@ -1120,11 +1247,11 @@
         0,
     )
     mel_gradient = mel_slots.reshape(S, piece_frames, mels)
-    return_w, hidden_w, output_w, query_w, key_w, value_w, reduce_w, short = [
-        v.astype(F32) for v in terms
-    ]
-    stem_w = short[: 3 * mels]
-    sums = short[used:]
+    rows = wide + 11
+    rows += -rows % 16
+    return_w, hidden_w, output_w, query_w, key_w, value_w, reduce_w, stem_w, sums = widen(
+        terms, (3 * mels, used), rows
+    )
     small = wide + 6
     return (
         layer_output,

time: 243 us -> 234 us (0.963)
  Pallas kernels: 154 us -> 169 us
  other arithmetic: 21.4 us -> 7.73 us
  starting transfers between devices: 8.96 us -> 0 us
  matrix products: 33.8 us -> 39.5 us
  waiting for transfers between devices: 3.49 us -> 0 us
  local copies, waits for them, and re-layouts: 18.2 us -> 15.1 us
    pallas_call x0 -> x2, Pallas kernels: none -> 16 us  [the longest x1 8.22 us: widen(): pl.pallas_call(functools.partial(widen_kernel, parts, len(arrays)), in_sp...]
    convert_element_type x9 -> x2, other arithmetic: 14.2 us -> 2.08 us  [the longest x1 1.78 us: on_device(): branch_grad = jnp.pad(mixed_grad.astype(BF16), ((0, R - T), (0, 0)))]
    ppermute x4 -> x0, starting transfers between devices: 8.96 us -> none  [the longest x2 4.9 us: gather_window(): got = lax.ppermute(part, 'frame', perm)]
    slice x3 -> x0, local copies, waits for them, and re-layouts: 4.24 us -> none  [the longest x1 2.45 us: on_device(): attended = attended_wide[:T].astype(BF16)]
    dot_general x3, matrix products: 10 us -> 13.7 us  [dot_t(): lax.dot_general(left, right, (((1,), (1,)), ((), ())), preferred_element_...]
    ppermute x4 -> x0, waiting for transfers between devices: 3.49 us -> none  [the longest x2 2.48 us: gather_window(): got = lax.ppermute(part, 'frame', perm)]
    unnamed x79 -> x75, local copies, waits for them, and re-layouts: 8.09 us -> 9.64 us
  transfers between devices with their start and end apart: 4 -> 0, of which waited for: 2 -> 0; matrix products, arithmetic and copies ran while one was open for 1% -> 0% of each run, Pallas kernels for 0% -> 0%
where the time goes in v2:
time: 234 us; the launch traced here: 233 us
  Pallas kernels  169 us (72%)
  matrix products  39.5 us (17%)
  local copies, waits for them, and re-layouts  15.1 us (6%)
  other arithmetic  7.73 us (3%)
    pallas_call x1, Pallas kernels, sum_everywhere(): pl.pallas_call(functools.partial(sum_kernel, sizes, F, used, plan), in_sp...  95.5 us
    pallas_call x1, Pallas kernels, attn_fwd(): pl.pallas_call(functools.partial(fwd_kernel, scale, hd, F, G, T, pairs),...  29 us
    pallas_call x1, Pallas kernels, attn_bwd(): pl.pallas_call(functools.partial(bwd_kernel, scale, hd, F, G, pairs), gri...  28.4 us
    dot_general x8, matrix products, dot(): return jnp.dot(left, right, preferred_element_type=F32)  25.8 us
    dot_general x3, matrix products, dot_t(): lax.dot_general(left, right, (((1,), (1,)), ((), ())), preferred_element_...  13.7 us
    unnamed x75, local copies, waits for them, and re-layouts  9.64 us
    pallas_call x1, Pallas kernels, widen(): pl.pallas_call(functools.partial(widen_kernel, parts, len(arrays)), in_sp...  8.22 us
    pallas_call x1, Pallas kernels, gather_mel(): pl.pallas_call(functools.partial(mel_kernel, F), in_specs=[far, far], out...  7.81 us

profile of v2, /device:TPU:0, one launch (start us, length us, event | category | flops | bytes accessed | tf_op | source)
XLA Modules:
  0.0 233.1 jit_solution(10664015688690046591)
XLA Ops:
  0.7 0.1 multiply_cosine_fusion.1
  0.9 0.3 multiply_sine_fusion
  1.1 1.4 multiply_add_fusion.4
  2.5 0.2 copy.46
  2.8 0.2 reshape.308.m_ref
  3.0 7.8 %shard_map.373 = (bf16[2,376,160]{2,1,0:T(8,128)(2,1)S(1)}, bf16[2,8,160]{2,1,0:T(8,128)(2,1)S(1)}) custom-call(bf16[2,376,160]{2,1,0:T(8,128)(2,1)S(1)} %reshape.308.m_ref, bf16[2,2,8,160]{3,2,1,0:T(8,128)(2,1)S(1)} %pad_maximum_fusion.7.e_ref), custom_call_target="tpu_custom_call" | custom-call | tf_op jit(solution)/shard_map/pallas_call | solution.py:240
  10.9 5.1 %fusion.5 = (bf16[768,1024]{1,0:T(8,128)(2,1)S(1)}, f32[768,1024]{1,0:T(8,128)}) fusion(pred[768]{0:T(1024)(128)(4,1)S(1)} %fusion.26, f32[1024]{0:T(1024)S(1)} %pad_maximum_fusion.8, bf16[240,512]{1,0:T(8,128)(2,1)S(1)} %bitcast.69, bf16[1,160]{1,0:T(2,128)(2,1)S(1)} %get-tuple-element.148, bf16[14,160]{1,0:T(8,128)(2,1)S(1)} %broadcast_in_dim.18, ...), kind=kOutput, calls=%fused_computation.15 | convolution fusion | flops 531988480 | bytes 5215296 | tf_op jit(solution)/shard_map/dot_general | solution.py:49
  16.0 0.1 slice.134
  16.3 1.0 copy-done.1
  17.3 0.2 pad_maximum_fusion.1.refs_10_
  17.4 0.6 copy-done.9
  18.0 0.2 copy-done.10
  18.2 0.2 copy-done.11
  18.4 3.9 %fusion.37 = (f32[752]{0:T(1024)S(1)}, f32[752,512]{1,0:T(8,128)S(1)}, f32[752,512]{1,0:T(8,128)}) fusion(f32[752,256]{1,0:T(8,128)S(1)} %bitcast.67, f32[752,256]{1,0:T(8,128)S(1)} %bitcast.66, f32[512]{0:T(512)S(1)} %copy-done.31, bf16[1536,512]{1,0:T(8,128)(2,1)S(1)} %bitcast.65, bf16[752,1024]{1,0:T(8,128)(2,1)S(1)} %slice.134, ...), kind=kOutput, calls=%fused_computation.99 | convolution fusion | flops 1197423872 | bytes 8508352 | tf_op jit(solution)/shard_map/dot_general | solution.py:49
  22.4 0.3 multiply_reduce_fusion.3
  22.8 0.3 copy-done.22
  23.1 0.3 add_convert_fusion.3
  23.4 0.5 copy-done.15
  24.0 1.4 add_convert_fusion.q_ref
  25.4 1.4 convolution_convert_fusion.1.k_own
  26.9 1.4 add_convert_fusion.2.v_own
  28.3 29.0 %shard_map.374 = (bf16[8,1504,768]{2,1,0:T(8,128)(2,1)}, f32[768,512]{1,0:T(8,128)}, bf16[768,512]{1,0:T(8,128)(2,1)}, bf16[1504,512]{1,0:T(8,128)(2,1)}, bf16[1...) custom-call(bf16[768,512]{1,0:T(8,128)(2,1)} %add_convert_fusion.q_ref, ...), custom_call_target="tpu_custom_call" | custom-call | tf_op jit(solution)/shard_map/pallas_call | solution.py:376
  57.3 1.8 fusion.41
  59.1 0.3 multiply_reduce_fusion.2
  59.5 0.3 copy-done.21
  59.8 0.3 add_convert_fusion.1.refs_2_
  60.1 1.0 copy-done.27
  61.1 8.1 %multiply_convert_fusion = (bf16[752,2048]{1,0:T(8,128)(2,1)}, f32[752,2048]{1,0:T(8,128)}) fusion(f32[2048]{0:T(1024)S(1)} %copy-done.30, bf16[752,512]{1,0:T(8,128)(2,1)S(1)} %add_convert_fusion.1.refs_2_, bf16[512,2048]{1,0:T(8,128)(2,1)S(1)} %copy-done.27), kind=kOutput, calls=%fused_computation.3 | convolution fusion | flops 1614020608 | bytes 12115968 | tf_op jit(solution)/shard_map/dot_general | solution.py:49
  69.9 9.5 %multiply_convert_fusion.1.refs_3_ = bf16[752,2048]{1,0:T(8,128)(2,1)S(1)} fusion(f32[752,2048]{1,0:T(8,128)} %get-tuple-element.159, bf16[752,512]{1,0:T(8,128)(2,1)S(1)} %bitcast.62, bf16[2048,512]{1,0:T(8,128)(2,1)} %param.41, f32[2048]{0:T(1024)S(1)} %copy-done.30), kind=kOutput, calls=%fused_computation.4 | convolution fusion | flops 1618640896 | bytes 12115968 | tf_op jit(solution)/shard_map/dot_general | solution.py:53
  79.4 2.8 %multiply_reduce_fusion = (f32[512]{0:T(512)}, f32[752]{0:T(1024)S(1)}, f32[752]{0:T(1024)S(1)}, f32[512]{0:T(512)}, f32[752,512]{1,0:T(8,128)S(1)}) fusion(f32[752,512]{1,0:T(8,128)S(1)} %get-tuple-element.157, f32[752]{0:T(1024)S(1)} %add_rsqrt_fusion, f32[752]{0:T(1024)S(1)} %broadcast_multiply_fusion.2, f32[512]{0:T(512)S(1)} %copy-done.21, ...), kind=kOutput, calls=%fused_computation.28 | convolution fusion | flops 1580520960 | bytes 8275712 | tf_op jit(solution)/shard_map/dot_general | solution.py:53
  82.2 1.8 fusion.36
  84.0 1.5 convolution_convert_fusion.do_ref
  85.5 0.3 copy-done.29
  85.8 2.6 %select_convert_fusion = bf16[752,512]{1,0:T(8,128)(2,1)} fusion(f32[752,512]{1,0:T(8,128)S(1)} %get-tuple-element.157, bf16[752,2048]{1,0:T(8,128)(2,1)S(1)} %copy-done.5, bf16[2048,512]{1,0:T(8,128)(2,1)S(1)} %copy-done.29, f32[512]{0:T(512)S(1)} %copy-done.34, pred[]{:T(512)S(6)} %lt.24), kind=kOutput, calls=%fused_computation.29 | convolution fusion | flops 1578598400 | bytes 7489537 | tf_op jit(solution)/shard_map/dot_general | solution.py:49
  88.4 28.4 %shard_map.375 = (bf16[768,512]{1,0:T(8,128)(2,1)}, bf16[752,512]{1,0:T(8,128)(2,1)}, bf16[752,512]{1,0:T(8,128)(2,1)}, bf16[2,376,512]{2,1,0:T(8,128)(2,1)}) custom-call(bf16[768,512]{1,0:T(8,128)(2,1)} %add_convert_fusion.q_ref, bf16[768,512]{1,0:T(8,128)(2,1)} %convolution_convert_fusion.do_ref, f32[768,512]{1,0:T(8,128)} %get-tuple-element.55.o_ref, ...), custom_call_target="tpu_custom_call" | custom-call | tf_op jit(solution)/shard_map/pallas_call | solution.py:530
  116.9 0.9 pad.12.refs_5_
  117.8 0.5 copy-done.4
  118.3 0.9 pad.11.refs_6_
  119.4 1.1 pad_maximum_fusion.refs_21_
  120.4 1.5 fusion.22.refs_22_
  121.9 95.5 %shard_map.376 = (bf16[2048,512]{1,0:T(8,128)(2,1)}, bf16[512,2048]{1,0:T(8,128)(2,1)}, bf16[512,512]{1,0:T(8,128)(2,1)}, bf16[512,512]{1,0:T(8,128)(2,1)}, bf16...) custom-call(bf16[752,2048]{1,0:T(8,128)(2,1)} %get-tuple-element.158, ...), custom_call_target="tpu_custom_call" | custom-call | tf_op jit(solution)/shard_map/pallas_call | solution.py:995
  217.5 1.3 reshape.315
  218.8 1.0 copy.47
  219.8 8.2 %shard_map.377 = (f32[2048,512]{1,0:T(8,128)}, f32[512,2048]{1,0:T(8,128)}, f32[512,512]{1,0:T(8,128)}, f32[512,512]{1,0:T(8,128)}, f32[512,512]{1,0:T(8,128)}, ...) custom-call(bf16[2048,512]{1,0:T(8,128)(2,1)} %get-tuple-element.64.refs_0_, ...), custom_call_target="tpu_custom_call" | custom-call | tf_op jit(solution)/shard_map/pallas_call | solution.py:1079
  228.0 1.7 fusion.40
  229.7 0.7 slice_bitcast_fusion.3
  230.4 0.6 copy.48
  231.0 2.0 copy.51
  (83 shorter events, 0.7 us)
Async XLA Ops:
  0.7 1.9 copy-start.26
  0.7 1.9 copy-start.18
  1.1 9.8 %copy-start.19 = (bf16[3,80,512]{2,1,0:T(8,128)(2,1)S(1)}, bf16[3,80,512]{2,1,0:T(8,128)(2,1)}, u32[]{:S(2)}) copy-start(bf16[3,80,512]{2,1,0:T(8,128)(2,1)} %param.24) | copy-start | bytes 737284
  16.0 1.2 copy-start.1
  16.1 1.9 copy-start.9
  16.2 2.0 copy-start.10
  16.2 2.3 copy-start.11
  16.2 2.3 copy-start.31
  18.4 3.9 %copy-start.8 = (bf16[752,512]{1,0:T(8,128)(2,1)}, bf16[752,512]{1,0:T(8,128)(2,1)S(1)}, u32[]{:S(2)}) copy-start(bf16[752,512]{1,0:T(8,128)(2,1)S(1)} %pad_maximum_fusion.1.refs_10_) | copy-start | bytes 2310148
  22.4 34.9 %copy-start = (f32[752,512]{1,0:T(8,128)}, f32[752,512]{1,0:T(8,128)S(1)}, u32[]{:S(2)}) copy-start(f32[752,512]{1,0:T(8,128)S(1)} %get-tuple-element.130.refs_15_) | copy-start | bytes 4620292
  22.4 0.7 copy-start.22
  22.4 0.7 copy-start.23
  22.7 1.2 copy-start.15
  22.7 1.2 copy-start.32
  24.0 2.9 %copy-start.3 = (bf16[752,512]{1,0:T(8,128)(2,1)}, bf16[752,512]{1,0:T(8,128)(2,1)S(1)}, u32[]{:S(2)}) copy-start(bf16[752,512]{1,0:T(8,128)(2,1)S(1)} %add_convert_fusion.3) | copy-start | bytes 2310148
  24.0 1.5 copy-start.16
  25.4 1.4 copy-start.17
  25.4 1.4 copy-start.33
  28.3 29.0 %copy-start.13 = (bf16[512,512]{1,0:T(8,128)(2,1)S(1)}, bf16[512,512]{1,0:T(8,128)(2,1)}, u32[]{:S(2)}) copy-start(bf16[512,512]{1,0:T(8,128)(2,1)} %param.35) | copy-start | bytes 1572868
  28.3 29.0 %copy-start.24 = (f32[512]{0:T(512)S(1)}, f32[512]{0:T(512)}, u32[]{:S(2)}) copy-start(f32[512]{0:T(512)} %param.36) | copy-start | bytes 6148
  59.1 0.7 copy-start.21
  59.1 0.7 copy-start.25
  59.5 1.6 copy-start.27
  59.5 1.6 copy-start.30
  61.1 8.1 %copy-start.7 = (bf16[752,512]{1,0:T(8,128)(2,1)}, bf16[752,512]{1,0:T(8,128)(2,1)S(1)}, u32[]{:S(2)}) copy-start(bf16[752,512]{1,0:T(8,128)(2,1)S(1)} %add_convert_fusion.1.refs_2_) | copy-start | bytes 2310148
  61.1 8.7 %copy-start.12 = (bf16[2,376,512]{2,1,0:T(8,128)(2,1)S(1)}, bf16[2,376,512]{2,1,0:T(8,128)(2,1)}, u32[]{:S(2)}) copy-start(bf16[2,376,512]{2,1,0:T(8,128)(2,1)} %get-tuple-element.53) | copy-start | bytes 2310148
  69.9 12.3 %copy-start.2 = (bf16[2,376,512]{2,1,0:T(8,128)(2,1)}, bf16[2,376,512]{2,1,0:T(8,128)(2,1)S(1)}, u32[]{:S(2)}) copy-start(bf16[2,376,512]{2,1,0:T(8,128)(2,1)S(1)} %broadcast_select_fusion) | copy-start | bytes 2310148
  69.9 9.5 %copy-start.28 = (bf16[512,2048]{1,0:T(8,128)(2,1)S(1)}, bf16[512,2048]{1,0:T(8,128)(2,1)}, u32[]{:S(2)}) copy-start(bf16[512,2048]{1,0:T(8,128)(2,1)} %param.39) | copy-start | bytes 6291460
  79.4 2.8 %copy-start.6 = (bf16[752,2048]{1,0:T(8,128)(2,1)}, bf16[752,2048]{1,0:T(8,128)(2,1)S(1)}, u32[]{:S(2)}) copy-start(bf16[752,2048]{1,0:T(8,128)(2,1)S(1)} %multiply_convert_fusion.1.refs_3_) | copy-start | bytes 9240580
  82.2 1.8 copy-start.14
  82.2 3.3 %copy-start.5 = (bf16[752,2048]{1,0:T(8,128)(2,1)S(1)}, bf16[752,2048]{1,0:T(8,128)(2,1)}, u32[]{:S(2)}) copy-start(bf16[752,2048]{1,0:T(8,128)(2,1)} %get-tuple-element.158.refs_0_) | copy-start | bytes 9240580
  84.0 1.8 copy-start.29
  84.0 1.8 copy-start.34
  116.8 1.4 copy-start.4
  116.9 2.3 %copy-start.20 = (bf16[3,80,512]{2,1,0:T(8,128)(2,1)S(1)}, bf16[3,80,512]{2,1,0:T(8,128)(2,1)}, u32[]{:S(2)}) copy-start(bf16[3,80,512]{2,1,0:T(8,128)(2,1)} %param.24) | copy-start | bytes 737284

commit v3 on v2

--- a/solution.py
+++ b/solution.py
@@ -555,7 +555,7 @@
 
 TILE = 512
 LAG = 3
-AHEAD = 3
+AHEAD = 2
 
 
 def pick(c, values):
@@ -875,7 +875,10 @@
             for o in range(1, sizes[k]):
                 copies[kind](c, k, o).start()
 
-    last = LAG * (len(stages) - 1) + AHEAD
+    turns = [AHEAD]
+    for n in range(1, len(stages)):
+        turns.append(turns[-1] + (LAG if stages[n][1] else LAG - 1))
+    last = turns[-1]
 
     def turn(t, _):
         for n in range(len(loads)):
@@ -908,7 +911,7 @@
                 scatter_copy(t - 1, 0, o).start()
 
         for n in range(len(stages) - 1, -1, -1):
-            c = t - AHEAD - LAG * n
+            c = t - turns[n]
 
             @pl.when((c >= 0) & (c < chunks))
             def _():
@@ -1158,10 +1161,11 @@
     conv_linear = dot(conv_columns, reduce_matrix) + reduce_bias
     stream = gelu(conv_linear) + positions_of(r * T, T, D)
     xhat1, r1 = norm_parts(stream)
-    first_normed = jnp.pad((xhat1 * first_gain + first_shift).astype(BF16), ((0, R - T), (0, 0)))
-    query_ext = (dot(first_normed, query_weight) + query_bias).astype(BF16)
-    key = dot(first_normed[:T], key_weight).astype(BF16)
-    value = (dot(first_normed[:T], value_weight) + value_bias).astype(BF16)
+    first_normed = (xhat1 * first_gain + first_shift).astype(BF16)
+    tail = ((0, R - T), (0, 0))
+    query_ext = (dot(jnp.pad(first_normed, tail), query_weight) + query_bias).astype(BF16)
+    key = dot(first_normed, key_weight).astype(BF16)
+    value = (dot(first_normed, value_weight) + value_bias).astype(BF16)
     key = jnp.pad(key, ((0, -T % 16), (0, 0)))
     value = jnp.pad(value, ((0, -T % 16), (0, 0)))
     block = 256 if R % 256 == 0 else 128
@@ -1185,9 +1189,9 @@
         xhat2, r2, second_gain, dot_t(hidden_grad, hidden_weight)
     )
     mixed_grad = cot.astype(F32) + inner
-    branch_grad = jnp.pad(mixed_grad.astype(BF16), ((0, R - T), (0, 0)))
-
-    attended_grad = dot_t(branch_grad, output_weight).astype(BF16)
+    branch_grad = mixed_grad.astype(BF16)
+
+    attended_grad = dot_t(jnp.pad(branch_grad, tail), output_weight).astype(BF16)
     query_wide, key_grad, value_grad, layer_output = attn_bwd(
         query_ext,
         attended_grad,

time: 234 us -> 231 us (0.987)
  no operation moved by 1% of the time
where the time goes in v3:
time: 231 us; the launch traced here: 230 us
  Pallas kernels  168 us (73%)
  matrix products  39.5 us (17%)
  local copies, waits for them, and re-layouts  13.3 us (6%)
  other arithmetic  7.72 us (3%)
    pallas_call x1, Pallas kernels, sum_everywhere(): pl.pallas_call(functools.partial(sum_kernel, sizes, F, used, plan), in_sp...  94.1 us
    pallas_call x1, Pallas kernels, attn_fwd(): pl.pallas_call(functools.partial(fwd_kernel, scale, hd, F, G, T, pairs),...  29 us
    pallas_call x1, Pallas kernels, attn_bwd(): pl.pallas_call(functools.partial(bwd_kernel, scale, hd, F, G, pairs), gri...  28.5 us
    dot_general x8, matrix products, dot(): return jnp.dot(left, right, preferred_element_type=F32)  25.8 us
    dot_general x3, matrix products, dot_t(): lax.dot_general(left, right, (((1,), (1,)), ((), ())), preferred_element_...  13.7 us
    unnamed x75, local copies, waits for them, and re-layouts  9.74 us
    pallas_call x1, Pallas kernels, widen(): pl.pallas_call(functools.partial(widen_kernel, parts, len(arrays)), in_sp...  8.22 us
    pallas_call x1, Pallas kernels, gather_mel(): pl.pallas_call(functools.partial(mel_kernel, F), in_specs=[far, far], out...  7.81 us

profile of v3, /device:TPU:0, one launch (start us, length us, event | category | flops | bytes accessed | tf_op | source)
XLA Modules:
  0.0 230.0 jit_solution(13528878231469887154)
XLA Ops:
  0.7 0.1 multiply_cosine_fusion.1
  0.9 0.3 multiply_sine_fusion
  1.1 1.4 multiply_add_fusion.4
  2.5 0.2 copy.46
  2.8 0.2 reshape.308.m_ref
  3.0 7.8 %shard_map.373 = (bf16[2,376,160]{2,1,0:T(8,128)(2,1)S(1)}, bf16[2,8,160]{2,1,0:T(8,128)(2,1)S(1)}) custom-call(bf16[2,376,160]{2,1,0:T(8,128)(2,1)S(1)} %reshape.308.m_ref, bf16[2,2,8,160]{3,2,1,0:T(8,128)(2,1)S(1)} %pad_maximum_fusion.7.e_ref), custom_call_target="tpu_custom_call" | custom-call | tf_op jit(solution)/shard_map/pallas_call | solution.py:240
  10.9 0.1 slice.128
  10.9 5.1 %fusion.5 = (bf16[768,1024]{1,0:T(8,128)(2,1)S(1)}, f32[768,1024]{1,0:T(8,128)}) fusion(pred[768]{0:T(1024)(128)(4,1)S(1)} %fusion.28, f32[1024]{0:T(1024)S(1)} %pad_maximum_fusion.8, bf16[240,512]{1,0:T(8,128)(2,1)S(1)} %bitcast.69, bf16[1,160]{1,0:T(2,128)(2,1)S(1)} %get-tuple-element.148, bf16[14,160]{1,0:T(8,128)(2,1)S(1)} %broadcast_in_dim.18, ...), kind=kOutput, calls=%fused_computation.15 | convolution fusion | flops 531988480 | bytes 5215296 | tf_op jit(solution)/shard_map/dot_general | solution.py:49
  16.0 0.1 slice.132
  16.2 0.1 slice.131
  16.3 1.0 copy-done.1
  17.3 0.2 pad_maximum_fusion.1.refs_10_
  17.4 0.6 copy-done.9
  18.0 0.2 copy-done.10
  18.2 0.2 copy-done.11
  18.4 3.9 %fusion.39 = (f32[752]{0:T(1024)S(1)}, f32[752,512]{1,0:T(8,128)S(1)}, f32[752,512]{1,0:T(8,128)}) fusion(f32[752,256]{1,0:T(8,128)S(1)} %bitcast.67, f32[752,256]{1,0:T(8,128)S(1)} %bitcast.66, f32[512]{0:T(512)S(1)} %copy-done.31, bf16[1536,512]{1,0:T(8,128)(2,1)S(1)} %bitcast.65, bf16[752,1024]{1,0:T(8,128)(2,1)S(1)} %slice.132, ...), kind=kOutput, calls=%fused_computation.101 | convolution fusion | flops 1197423872 | bytes 8508352 | tf_op jit(solution)/shard_map/dot_general | solution.py:49
  22.4 0.3 multiply_reduce_fusion.3
  22.8 0.3 copy-done.22
  23.0 0.1 copy-done.23
  23.1 0.3 add_convert_fusion.3.refs_6_
  23.4 0.5 copy-done.15
  24.0 1.4 add_convert_fusion.q_ref
  25.4 1.4 convolution_convert_fusion.1.k_own
  26.9 1.4 add_convert_fusion.2.v_own
  28.3 29.0 %shard_map.374 = (bf16[8,1504,768]{2,1,0:T(8,128)(2,1)}, f32[768,512]{1,0:T(8,128)}, bf16[768,512]{1,0:T(8,128)(2,1)}, bf16[1504,512]{1,0:T(8,128)(2,1)}, bf16[1...) custom-call(bf16[768,512]{1,0:T(8,128)(2,1)} %add_convert_fusion.q_ref, ...), custom_call_target="tpu_custom_call" | custom-call | tf_op jit(solution)/shard_map/pallas_call | solution.py:376
  57.3 1.8 fusion.43
  59.1 0.3 multiply_reduce_fusion.2
  59.5 0.3 copy-done.21
  59.8 0.3 add_convert_fusion.1.refs_2_
  60.1 1.0 copy-done.27
  61.1 8.1 %multiply_convert_fusion = (bf16[752,2048]{1,0:T(8,128)(2,1)}, f32[752,2048]{1,0:T(8,128)}) fusion(f32[2048]{0:T(1024)S(1)} %copy-done.30, bf16[752,512]{1,0:T(8,128)(2,1)S(1)} %add_convert_fusion.1.refs_2_, bf16[512,2048]{1,0:T(8,128)(2,1)S(1)} %copy-done.27), kind=kOutput, calls=%fused_computation.3 | convolution fusion | flops 1614020608 | bytes 12115968 | tf_op jit(solution)/shard_map/dot_general | solution.py:49
  69.9 9.5 %multiply_convert_fusion.1.refs_3_ = bf16[752,2048]{1,0:T(8,128)(2,1)S(1)} fusion(f32[752,2048]{1,0:T(8,128)} %get-tuple-element.159, bf16[752,512]{1,0:T(8,128)(2,1)S(1)} %bitcast.62, bf16[2048,512]{1,0:T(8,128)(2,1)} %param.41, f32[2048]{0:T(1024)S(1)} %copy-done.30), kind=kOutput, calls=%fused_computation.4 | convolution fusion | flops 1618640896 | bytes 12115968 | tf_op jit(solution)/shard_map/dot_general | solution.py:53
  79.4 2.7 %multiply_reduce_fusion = (f32[512]{0:T(512)}, f32[752]{0:T(1024)S(1)}, f32[752]{0:T(1024)S(1)}, f32[512]{0:T(512)}, f32[752,512]{1,0:T(8,128)S(1)}) fusion(f32[752,512]{1,0:T(8,128)S(1)} %get-tuple-element.157, f32[752]{0:T(1024)S(1)} %add_rsqrt_fusion, f32[752]{0:T(1024)S(1)} %broadcast_multiply_fusion.2, f32[512]{0:T(512)S(1)} %copy-done.21, ...), kind=kOutput, calls=%fused_computation.28 | convolution fusion | flops 1580520960 | bytes 8275712 | tf_op jit(solution)/shard_map/dot_general | solution.py:53
  82.2 1.8 fusion.38
  83.9 1.5 convolution_convert_fusion.do_ref
  85.4 0.9 copy-done.29
  86.3 2.7 %select_convert_fusion = bf16[752,512]{1,0:T(8,128)(2,1)} fusion(f32[752,512]{1,0:T(8,128)S(1)} %get-tuple-element.157, bf16[752,2048]{1,0:T(8,128)(2,1)S(1)} %copy-done.3, bf16[2048,512]{1,0:T(8,128)(2,1)S(1)} %copy-done.29, f32[512]{0:T(512)S(1)} %copy-done.34, pred[]{:T(512)S(6)} %lt.24), kind=kOutput, calls=%fused_computation.29 | convolution fusion | flops 1578598400 | bytes 7489537 | tf_op jit(solution)/shard_map/dot_general | solution.py:49
  88.9 28.5 %shard_map.375 = (bf16[768,512]{1,0:T(8,128)(2,1)}, bf16[752,512]{1,0:T(8,128)(2,1)}, bf16[752,512]{1,0:T(8,128)(2,1)}, bf16[2,376,512]{2,1,0:T(8,128)(2,1)}) custom-call(bf16[768,512]{1,0:T(8,128)(2,1)} %add_convert_fusion.q_ref, bf16[768,512]{1,0:T(8,128)(2,1)} %convolution_convert_fusion.do_ref, f32[768,512]{1,0:T(8,128)} %get-tuple-element.55.o_ref, ...), custom_call_target="tpu_custom_call" | custom-call | tf_op jit(solution)/shard_map/pallas_call | solution.py:530
  117.6 1.1 pad_maximum_fusion.refs_21_
  118.7 1.5 fusion.24.refs_22_
  120.2 94.1 %shard_map.376 = (bf16[2048,512]{1,0:T(8,128)(2,1)}, bf16[512,2048]{1,0:T(8,128)(2,1)}, bf16[512,512]{1,0:T(8,128)(2,1)}, bf16[512,512]{1,0:T(8,128)(2,1)}, bf16...) custom-call(bf16[752,2048]{1,0:T(8,128)(2,1)} %get-tuple-element.158, ...), custom_call_target="tpu_custom_call" | custom-call | tf_op jit(solution)/shard_map/pallas_call | solution.py:998
  214.3 1.3 reshape.315
  215.6 1.0 copy.47
  216.7 8.2 %shard_map.377 = (f32[2048,512]{1,0:T(8,128)}, f32[512,2048]{1,0:T(8,128)}, f32[512,512]{1,0:T(8,128)}, f32[512,512]{1,0:T(8,128)}, f32[512,512]{1,0:T(8,128)}, ...) custom-call(bf16[2048,512]{1,0:T(8,128)(2,1)} %get-tuple-element.64.refs_0_, ...), custom_call_target="tpu_custom_call" | custom-call | tf_op jit(solution)/shard_map/pallas_call | solution.py:1082
  224.9 1.7 fusion.42
  226.6 0.7 slice_bitcast_fusion.3
  227.3 0.6 copy.48
  227.9 2.0 copy.51
  (81 shorter events, 0.5 us)
Async XLA Ops:
  0.7 1.9 copy-start.26
  0.7 1.9 copy-start.18
  1.1 9.8 %copy-start.19 = (bf16[3,80,512]{2,1,0:T(8,128)(2,1)S(1)}, bf16[3,80,512]{2,1,0:T(8,128)(2,1)}, u32[]{:S(2)}) copy-start(bf16[3,80,512]{2,1,0:T(8,128)(2,1)} %param.24) | copy-start | bytes 737284
  16.0 1.2 copy-start.1
  16.1 1.9 copy-start.9
  16.2 2.0 copy-start.10
  16.2 2.3 copy-start.11
  16.2 2.3 copy-start.31
  18.4 3.9 %copy-start.7 = (bf16[752,512]{1,0:T(8,128)(2,1)}, bf16[752,512]{1,0:T(8,128)(2,1)S(1)}, u32[]{:S(2)}) copy-start(bf16[752,512]{1,0:T(8,128)(2,1)S(1)} %pad_maximum_fusion.1.refs_10_) | copy-start | bytes 2310148
  22.4 34.9 %copy-start = (f32[752,512]{1,0:T(8,128)}, f32[752,512]{1,0:T(8,128)S(1)}, u32[]{:S(2)}) copy-start(f32[752,512]{1,0:T(8,128)S(1)} %get-tuple-element.130.refs_15_) | copy-start | bytes 4620292
  22.4 0.7 copy-start.22
  22.4 0.7 copy-start.23
  22.7 1.2 copy-start.15
  22.7 1.2 copy-start.32
  24.0 2.9 %copy-start.5 = (bf16[752,512]{1,0:T(8,128)(2,1)}, bf16[752,512]{1,0:T(8,128)(2,1)S(1)}, u32[]{:S(2)}) copy-start(bf16[752,512]{1,0:T(8,128)(2,1)S(1)} %add_convert_fusion.3.refs_6_) | copy-start | bytes 2310148
  24.0 1.5 copy-start.16
  25.4 1.4 copy-start.17
  25.4 1.4 copy-start.33
  28.3 29.0 %copy-start.13 = (bf16[512,512]{1,0:T(8,128)(2,1)S(1)}, bf16[512,512]{1,0:T(8,128)(2,1)}, u32[]{:S(2)}) copy-start(bf16[512,512]{1,0:T(8,128)(2,1)} %param.35) | copy-start | bytes 1572868
  28.3 29.0 %copy-start.24 = (f32[512]{0:T(512)S(1)}, f32[512]{0:T(512)}, u32[]{:S(2)}) copy-start(f32[512]{0:T(512)} %param.36) | copy-start | bytes 6148
  59.1 0.7 copy-start.21
  59.1 0.7 copy-start.25
  59.5 1.6 copy-start.27
  59.5 1.6 copy-start.30
  61.1 8.1 %copy-start.6 = (bf16[752,512]{1,0:T(8,128)(2,1)}, bf16[752,512]{1,0:T(8,128)(2,1)S(1)}, u32[]{:S(2)}) copy-start(bf16[752,512]{1,0:T(8,128)(2,1)S(1)} %add_convert_fusion.1.refs_2_) | copy-start | bytes 2310148
  61.1 8.7 %copy-start.12 = (bf16[2,376,512]{2,1,0:T(8,128)(2,1)S(1)}, bf16[2,376,512]{2,1,0:T(8,128)(2,1)}, u32[]{:S(2)}) copy-start(bf16[2,376,512]{2,1,0:T(8,128)(2,1)} %get-tuple-element.53) | copy-start | bytes 2310148
  69.9 12.2 %copy-start.2 = (bf16[2,376,512]{2,1,0:T(8,128)(2,1)}, bf16[2,376,512]{2,1,0:T(8,128)(2,1)S(1)}, u32[]{:S(2)}) copy-start(bf16[2,376,512]{2,1,0:T(8,128)(2,1)S(1)} %broadcast_select_fusion) | copy-start | bytes 2310148
  69.9 9.5 %copy-start.28 = (bf16[512,2048]{1,0:T(8,128)(2,1)S(1)}, bf16[512,2048]{1,0:T(8,128)(2,1)}, u32[]{:S(2)}) copy-start(bf16[512,2048]{1,0:T(8,128)(2,1)} %param.39) | copy-start | bytes 6291460
  79.4 2.7 %copy-start.4 = (bf16[752,2048]{1,0:T(8,128)(2,1)}, bf16[752,2048]{1,0:T(8,128)(2,1)S(1)}, u32[]{:S(2)}) copy-start(bf16[752,2048]{1,0:T(8,128)(2,1)S(1)} %multiply_convert_fusion.1.refs_3_) | copy-start | bytes 9240580
  82.1 1.8 copy-start.14
  82.1 3.3 %copy-start.3 = (bf16[752,2048]{1,0:T(8,128)(2,1)S(1)}, bf16[752,2048]{1,0:T(8,128)(2,1)}, u32[]{:S(2)}) copy-start(bf16[752,2048]{1,0:T(8,128)(2,1)} %get-tuple-element.158.refs_0_) | copy-start | bytes 9240580
  83.9 5.0 %copy-start.8 = (bf16[752,512]{1,0:T(8,128)(2,1)}, bf16[752,512]{1,0:T(8,128)(2,1)S(1)}, u32[]{:S(2)}) copy-start(bf16[752,512]{1,0:T(8,128)(2,1)S(1)} %get-tuple-element.127.refs_5_) | copy-start | bytes 2310148
  83.9 2.4 %copy-start.29 = (bf16[2048,512]{1,0:T(8,128)(2,1)S(1)}, bf16[2048,512]{1,0:T(8,128)(2,1)}, u32[]{:S(2)}) copy-start(bf16[2048,512]{1,0:T(8,128)(2,1)} %param.41) | copy-start | bytes 6291460
  83.9 2.4 %copy-start.34 = (f32[512]{0:T(512)S(1)}, f32[512]{0:T(512)}, u32[]{:S(2)}) copy-start(f32[512]{0:T(512)} %param.42) | copy-start | bytes 6148
  88.9 28.5 %copy-start.20 = (bf16[3,80,512]{2,1,0:T(8,128)(2,1)S(1)}, bf16[3,80,512]{2,1,0:T(8,128)(2,1)}, u32[]{:S(2)}) copy-start(bf16[3,80,512]{2,1,0:T(8,128)(2,1)} %param.24) | copy-start | bytes 737284
